TPU v7x, 32 devices: a whole 2x2x4 slice. The times are simulated.
32 devices in a mesh: wave: 4 (over y, x), event: 8 (over z, core).
Axes of the slice: x: 2, y: 2, z: 4, core: 2. Of those that a mesh axis runs over, the one named last changes fastest.
Arguments:
- latent: bfloat16 [8, 512, 2048], P(None, 'wave', 'event'), may hold values from -6 to 6
- basis: bfloat16 [262144, 512], P('event', 'wave'), may hold values from -0.29882812 to 0.29882812
- event_bin: int32 [8, 32768], P('event'), may hold values from 0 to 255, never falling along the last dimension, each value on 1 to 512 neighbouring positions
- length: float32 [512, 2048], P('wave', 'event'), may hold values from 0.01 to 0.08
- amplitude_scale: float32 [512, 2048], P('wave', 'event'), may hold values from 0.3 to 1
- yield_norm: float32 [512, 2048], P('wave', 'event'), may hold values from 0.5 to 2
- bin_coords: float32 [2, 2048], replicated, may hold values from 0 to 1
Outputs:
- grad_latent: float32 [8, 512, 2048], P(None, 'wave', 'event')
Inputs may be any that keep to these rules, and one draw needn't show every extreme that they name: `event_bin`: along each block's events, bin numbers never fall and every one of the block's bins holds at least one event.
All inputs are finite; a program needn't handle non-finite values.
Results may differ from a plain program's by a relative error of at most 0.0024.
Values may be sent and summed in bfloat16 or wider, within the bound.
A program may use at most 256 MiB of HBM per device.

v0:
```python
import jax
import jax.numpy as jnp
from jax import lax
from jax.sharding import PartitionSpec as P


def gibbs(rows_xy, cols_xy, len_rows, amp_rows, len_cols, amp_cols):
    diff_x = rows_xy[0][:, None] - cols_xy[0][None, :]
    diff_y = rows_xy[1][:, None] - cols_xy[1][None, :]
    dist = diff_x * diff_x + diff_y * diff_y
    left = len_rows[:, :, None]
    right = len_cols[:, None, :]
    spread = left * left + right * right
    return (
        amp_rows[:, :, None]
        * amp_cols[:, None, :]
        * jnp.sqrt(2.0 * (left * right) / spread)
        * jnp.exp(-dist / spread)
    )


def shards(latent, basis, event_bin, length, amplitude_scale, yield_norm, bin_coords):
    position = lax.axis_index("event")
    waves = length.shape[0]
    rows = length.shape[1]
    samples = latent.shape[0]
    total_bins = bin_coords.shape[1]
    len_all, amp_all = (
        lax.all_gather(length, "event", axis=1, tiled=True),
        lax.all_gather(amplitude_scale, "event", axis=1, tiled=True),
    )
    rows_xy = lax.dynamic_slice_in_dim(bin_coords, position * rows, rows, 1)
    group = min(waves, 16)

    def split_waves(values):
        return values.reshape(waves // group, group, values.shape[1])

    def build(pieces):
        len_rows, amp_rows, len_cols, amp_cols = pieces
        return gibbs(rows_xy, bin_coords, len_rows, amp_rows, len_cols, amp_cols).astype(
            jnp.bfloat16
        )

    kern = lax.map(
        build,
        (
            split_waves(length),
            split_waves(amplitude_scale),
            split_waves(len_all),
            split_waves(amp_all),
        ),
    )
    kern = kern.reshape(waves, rows, total_bins)
    columns = kern
    amp_field = jnp.einsum(
        "wrc,swc->swr",
        columns,
        lax.all_gather(latent, "event", axis=2, tiled=True),
        preferred_element_type=jnp.float32,
    ).astype(jnp.bfloat16)
    amp_rows = jnp.transpose(amp_field, (2, 0, 1)).reshape(rows, samples * waves)
    events = basis.shape[0]
    block = min(events, 2048)
    count = events // block
    basis_blocks = basis.reshape(count, block, waves)
    bin_blocks = event_bin.reshape(count, block)
    labels = jnp.arange(rows, dtype=jnp.int32)

    def forward(pieces):
        psi, seg = pieces
        onehot = (seg[:, None] == labels[None, :]).astype(jnp.bfloat16)
        picked = jnp.dot(onehot, amp_rows, preferred_element_type=jnp.float32).reshape(
            block, samples, waves
        )
        return jnp.sum(picked * psi.astype(jnp.float32)[:, None, :], axis=2).T

    partial_fields = lax.map(forward, (basis_blocks, bin_blocks))
    fields = lax.psum(partial_fields, "wave")

    def backward(total, pieces):
        psi, seg, field = pieces
        weight = -2.0 * field / (1.0 + field * field) / samples
        terms = (weight.T[:, :, None] * psi.astype(jnp.float32)[:, None, :]).astype(jnp.bfloat16)
        terms = terms.reshape(block, samples * waves)
        onehot = (seg[:, None] == labels[None, :]).astype(jnp.bfloat16)
        added = lax.dot_general(
            onehot, terms, (((0,), (0,)), ((), ())), preferred_element_type=jnp.float32
        )
        return (total + added, None)

    start_sums = jnp.zeros((rows, samples * waves), jnp.float32)
    sums, unused = lax.scan(backward, start_sums, (basis_blocks, bin_blocks, fields))
    yield_term = 2.0 / samples * amp_field.astype(jnp.float32) * yield_norm[None]
    yield_rows = jnp.transpose(yield_term, (2, 0, 1)).reshape(rows, samples * waves)
    grad_rows = (sums + yield_rows).astype(jnp.bfloat16)
    piece = lax.all_gather(grad_rows, "event", axis=0, tiled=True)
    size = piece.shape[0]
    columns = kern
    pulled = jnp.einsum(
        "wrc,csw->swr",
        columns,
        piece.reshape(size, samples, waves),
        preferred_element_type=jnp.float32,
    )
    return pulled + latent.astype(jnp.float32)


def solution(mesh):
    placed = (
        P(None, "wave", "event"),
        P("event", "wave"),
        P("event", None),
        P("wave", "event"),
        P("wave", "event"),
        P("wave", "event"),
        P(),
    )
    return jax.shard_map(
        shards, mesh=mesh, in_specs=placed, out_specs=P(None, "wave", "event"), check_vma=False
    )
```

profile of v0, /device:TPU:0, one launch (start us, length us, event | category | flops | bytes accessed | tf_op | source)
XLA Modules:
  0.0 854.4 jit_solution(5387432393529406269)
XLA Ops:
  14.3 19.6 %all-gather.7.cloned.1.call-done = f32[128,2048]{1,0:T(8,128)} async-done(((f32[128,256]{1,0:T(8,128)}), f32[128,2048]{1,0:T(8,128)}) %all-gather.7.cloned.1.call-update) | async-done | bytes 1048592 | tf_op jit(solution)/shard_map/all_gather | solution.py:29
  33.9 23.5 %all-gather.5.cloned.1.call-done = f32[128,2048]{1,0:T(8,128)} async-done(((f32[128,256]{1,0:T(8,128)}), f32[128,2048]{1,0:T(8,128)}) %all-gather.5.cloned.1.call-update) | async-done | bytes 1048592 | tf_op jit(solution)/shard_map/all_gather | solution.py:30
  57.4 268.9 %while.32 = (s32[]{:T(128)}, bf16[8,16,256,2048]{3,2,1,0:T(8,128)(2,1)}, f32[8,16,256]{2,1,0:T(8,128)}, f32[8,16,2048]{2,1,0:T(8,128)}, f32[8,16,256]{2,1,0:T(8,...) while((s32[]{:T(128)}, ...), condition=%wide.region_1.2_spmd, body=%wide.region_0.1_spmd.sunk | while | flops 78680064 | bytes 22207084 | solution.py:44
  62.0 29.0 %fusion.49 = bf16[8,16,256,2048]{3,2,1,0:T(8,128)(2,1)} fusion(bf16[8,16,256,2048]{3,2,1,0:T(8,128)(2,1)} %get-tuple-element.339, s32[]{:T(128)} %get-tuple-element.338, f32[256,2048]{1,0:T(8,128)S(1)} %add_negate_fusion.2, f32[16,2048]{1,0:T(8,128)S(1)} %get-tuple-element.315, f32[16,256]{1,0:T(8,128)S(1)} %get-tuple-element.316, ...), kind=kLoop, calls=%fused_computation.9.clone.1 | loop fusion | flops 75497472 | bytes 19317248 | tf_op jit(solution)/shard_map/while/body/jit(dynamic_update_index_in_dim)/dynamic_update_slice | solution.py:44
  95.7 29.0 %fusion.49 = bf16[8,16,256,2048]{3,2,1,0:T(8,128)(2,1)} fusion(bf16[8,16,256,2048]{3,2,1,0:T(8,128)(2,1)} %get-tuple-element.339, s32[]{:T(128)} %get-tuple-element.338, f32[256,2048]{1,0:T(8,128)S(1)} %add_negate_fusion.2, f32[16,2048]{1,0:T(8,128)S(1)} %get-tuple-element.315, f32[16,256]{1,0:T(8,128)S(1)} %get-tuple-element.316, ...), kind=kLoop, calls=%fused_computation.9.clone.1 | loop fusion | flops 75497472 | bytes 19317248 | tf_op jit(solution)/shard_map/while/body/jit(dynamic_update_index_in_dim)/dynamic_update_slice | solution.py:44
  129.3 29.0 %fusion.49 = bf16[8,16,256,2048]{3,2,1,0:T(8,128)(2,1)} fusion(bf16[8,16,256,2048]{3,2,1,0:T(8,128)(2,1)} %get-tuple-element.339, s32[]{:T(128)} %get-tuple-element.338, f32[256,2048]{1,0:T(8,128)S(1)} %add_negate_fusion.2, f32[16,2048]{1,0:T(8,128)S(1)} %get-tuple-element.315, f32[16,256]{1,0:T(8,128)S(1)} %get-tuple-element.316, ...), kind=kLoop, calls=%fused_computation.9.clone.1 | loop fusion | flops 75497472 | bytes 19317248 | tf_op jit(solution)/shard_map/while/body/jit(dynamic_update_index_in_dim)/dynamic_update_slice | solution.py:44
  162.9 29.0 %fusion.49 = bf16[8,16,256,2048]{3,2,1,0:T(8,128)(2,1)} fusion(bf16[8,16,256,2048]{3,2,1,0:T(8,128)(2,1)} %get-tuple-element.339, s32[]{:T(128)} %get-tuple-element.338, f32[256,2048]{1,0:T(8,128)S(1)} %add_negate_fusion.2, f32[16,2048]{1,0:T(8,128)S(1)} %get-tuple-element.315, f32[16,256]{1,0:T(8,128)S(1)} %get-tuple-element.316, ...), kind=kLoop, calls=%fused_computation.9.clone.1 | loop fusion | flops 75497472 | bytes 19317248 | tf_op jit(solution)/shard_map/while/body/jit(dynamic_update_index_in_dim)/dynamic_update_slice | solution.py:44
  196.5 29.0 %fusion.49 = bf16[8,16,256,2048]{3,2,1,0:T(8,128)(2,1)} fusion(bf16[8,16,256,2048]{3,2,1,0:T(8,128)(2,1)} %get-tuple-element.339, s32[]{:T(128)} %get-tuple-element.338, f32[256,2048]{1,0:T(8,128)S(1)} %add_negate_fusion.2, f32[16,2048]{1,0:T(8,128)S(1)} %get-tuple-element.315, f32[16,256]{1,0:T(8,128)S(1)} %get-tuple-element.316, ...), kind=kLoop, calls=%fused_computation.9.clone.1 | loop fusion | flops 75497472 | bytes 19317248 | tf_op jit(solution)/shard_map/while/body/jit(dynamic_update_index_in_dim)/dynamic_update_slice | solution.py:44
  230.1 29.0 %fusion.49 = bf16[8,16,256,2048]{3,2,1,0:T(8,128)(2,1)} fusion(bf16[8,16,256,2048]{3,2,1,0:T(8,128)(2,1)} %get-tuple-element.339, s32[]{:T(128)} %get-tuple-element.338, f32[256,2048]{1,0:T(8,128)S(1)} %add_negate_fusion.2, f32[16,2048]{1,0:T(8,128)S(1)} %get-tuple-element.315, f32[16,256]{1,0:T(8,128)S(1)} %get-tuple-element.316, ...), kind=kLoop, calls=%fused_computation.9.clone.1 | loop fusion | flops 75497472 | bytes 19317248 | tf_op jit(solution)/shard_map/while/body/jit(dynamic_update_index_in_dim)/dynamic_update_slice | solution.py:44
  263.7 29.0 %fusion.49 = bf16[8,16,256,2048]{3,2,1,0:T(8,128)(2,1)} fusion(bf16[8,16,256,2048]{3,2,1,0:T(8,128)(2,1)} %get-tuple-element.339, s32[]{:T(128)} %get-tuple-element.338, f32[256,2048]{1,0:T(8,128)S(1)} %add_negate_fusion.2, f32[16,2048]{1,0:T(8,128)S(1)} %get-tuple-element.315, f32[16,256]{1,0:T(8,128)S(1)} %get-tuple-element.316, ...), kind=kLoop, calls=%fused_computation.9.clone.1 | loop fusion | flops 75497472 | bytes 19317248 | tf_op jit(solution)/shard_map/while/body/jit(dynamic_update_index_in_dim)/dynamic_update_slice | solution.py:44
  297.3 29.0 %fusion.49 = bf16[8,16,256,2048]{3,2,1,0:T(8,128)(2,1)} fusion(bf16[8,16,256,2048]{3,2,1,0:T(8,128)(2,1)} %get-tuple-element.339, s32[]{:T(128)} %get-tuple-element.338, f32[256,2048]{1,0:T(8,128)S(1)} %add_negate_fusion.2, f32[16,2048]{1,0:T(8,128)S(1)} %get-tuple-element.315, f32[16,256]{1,0:T(8,128)S(1)} %get-tuple-element.316, ...), kind=kLoop, calls=%fused_computation.9.clone.1 | loop fusion | flops 75497472 | bytes 19317248 | tf_op jit(solution)/shard_map/while/body/jit(dynamic_update_index_in_dim)/dynamic_update_slice | solution.py:44
  326.3 47.5 %convert_multiply_fusion = (f32[256,8,128]{0,1,2:T(8,128)S(1)}, bf16[256,8,128]{0,1,2:T(8,128)(2,1)S(1)}) fusion(f32[256,128]{0,1:T(8,128)S(1)} %multiply_bitcast_fusion.1, bf16[128,256,2048]{2,1,0:T(8,128)(2,1)} %bitcast.12, bf16[8,128,2048]{2,0,1:T(8,128)(2,1)} %all-gather.9.cloned.1.call-done), kind=kOutput, calls=%fused_computation.41 | convolution fusion | flops 1074528256 | bytes 140115968 | tf_op jit(solution)/shard_map/wrc,swc->swr/dot_general | solution.py:55
  374.2 64.0 %while.33 = (s32[]{:T(128)}, f32[16,8,2048]{2,1,0:T(8,128)}, s32[16,2048]{1,0:T(8,128)S(1)}, bf16[256,1024]{1,0:T(8,128)(2,1)S(1)}, bf16[16,2048,128]{2,1,0:T(8,128)(2,1)}, /*index=5*/s32[]{:T(128)}) while((s32[]{:T(128)}, f32[16,8,2048]{2,1,0:T(8,128)}, s32[16,2048]{1,0:T(8,128)S(1)}, bf16[256,1024]{1,0:T(8,128)(2,1)S(1)}, ...), condition=%wide.region_4.5_spmd.clone, body=%wide.region_2.4_spmd.clone.sunk | while | flops 1078706176 | bytes 5464653 | solution.py:77
  438.7 51.6 %all-reduce.2.cloned.1.call-done = f32[16,8,2048]{2,1,0:T(8,128)} async-done(((f32[16,8,2048]{2,1,0:T(8,128)}), f32[16,8,2048]{2,1,0:T(8,128)}) %all-reduce.2.cloned.1.call-update) | async-done | bytes 1048592 | tf_op jit(solution)/shard_map/psum | solution.py:78
  490.4 257.2 %while.34 = (s32[]{:T(128)}, f32[256,1024]{1,0:T(8,128)}, s32[16,2048]{1,0:T(8,128)S(1)}, f32[16,8,2048]{2,1,0:T(8,128)}, bf16[16,2048,128]{2,1,0:T(8,128)(2,1)}, /*index=5*/s32[]{:T(128)}, s32[]{:T(128)}) while((s32[]{:T(128)}, f32[256,1024]{1,0:T(8,128)}, s32[16,2048]{1,0:T(8,128)S(1)}, f32[16,8,2048]{2,1,0:T(8,128)}, ...), condition=%wide.region_7.8_spmd.clone, body=%wide.region_6.7_spmd.clone.sunk | while | flops 1079328768 | bytes 13459555 | solution.py:92
  492.8 8.6 %multiply_convert_fusion.2 = bf16[2048,8,128]{2,1,0:T(8,128)(2,1)} fusion(f32[2048,128]{1,0:T(8,128)S(1)} %bitcast_convert_fusion.5, f32[2048,8]{1,0:T(8,128)S(1)} %copy.43), kind=kLoop, calls=%fused_computation.23.clone.1 | loop fusion | flops 4194304 | bytes 5308416 | tf_op jit(solution)/shard_map/while/body/eval_jaxpr/convert_element_type | solution.py:83
  508.5 8.6 %multiply_convert_fusion.2 = bf16[2048,8,128]{2,1,0:T(8,128)(2,1)} fusion(f32[2048,128]{1,0:T(8,128)S(1)} %bitcast_convert_fusion.5, f32[2048,8]{1,0:T(8,128)S(1)} %copy.43), kind=kLoop, calls=%fused_computation.23.clone.1 | loop fusion | flops 4194304 | bytes 5308416 | tf_op jit(solution)/shard_map/while/body/eval_jaxpr/convert_element_type | solution.py:83
  524.6 8.6 %multiply_convert_fusion.2 = bf16[2048,8,128]{2,1,0:T(8,128)(2,1)} fusion(f32[2048,128]{1,0:T(8,128)S(1)} %bitcast_convert_fusion.5, f32[2048,8]{1,0:T(8,128)S(1)} %copy.43), kind=kLoop, calls=%fused_computation.23.clone.1 | loop fusion | flops 4194304 | bytes 5308416 | tf_op jit(solution)/shard_map/while/body/eval_jaxpr/convert_element_type | solution.py:83
  540.7 8.6 %multiply_convert_fusion.2 = bf16[2048,8,128]{2,1,0:T(8,128)(2,1)} fusion(f32[2048,128]{1,0:T(8,128)S(1)} %bitcast_convert_fusion.5, f32[2048,8]{1,0:T(8,128)S(1)} %copy.43), kind=kLoop, calls=%fused_computation.23.clone.1 | loop fusion | flops 4194304 | bytes 5308416 | tf_op jit(solution)/shard_map/while/body/eval_jaxpr/convert_element_type | solution.py:83
  556.8 8.6 %multiply_convert_fusion.2 = bf16[2048,8,128]{2,1,0:T(8,128)(2,1)} fusion(f32[2048,128]{1,0:T(8,128)S(1)} %bitcast_convert_fusion.5, f32[2048,8]{1,0:T(8,128)S(1)} %copy.43), kind=kLoop, calls=%fused_computation.23.clone.1 | loop fusion | flops 4194304 | bytes 5308416 | tf_op jit(solution)/shard_map/while/body/eval_jaxpr/convert_element_type | solution.py:83
  572.9 8.6 %multiply_convert_fusion.2 = bf16[2048,8,128]{2,1,0:T(8,128)(2,1)} fusion(f32[2048,128]{1,0:T(8,128)S(1)} %bitcast_convert_fusion.5, f32[2048,8]{1,0:T(8,128)S(1)} %copy.43), kind=kLoop, calls=%fused_computation.23.clone.1 | loop fusion | flops 4194304 | bytes 5308416 | tf_op jit(solution)/shard_map/while/body/eval_jaxpr/convert_element_type | solution.py:83
  589.0 8.6 %multiply_convert_fusion.2 = bf16[2048,8,128]{2,1,0:T(8,128)(2,1)} fusion(f32[2048,128]{1,0:T(8,128)S(1)} %bitcast_convert_fusion.5, f32[2048,8]{1,0:T(8,128)S(1)} %copy.43), kind=kLoop, calls=%fused_computation.23.clone.1 | loop fusion | flops 4194304 | bytes 5308416 | tf_op jit(solution)/shard_map/while/body/eval_jaxpr/convert_element_type | solution.py:83
  605.1 8.6 %multiply_convert_fusion.2 = bf16[2048,8,128]{2,1,0:T(8,128)(2,1)} fusion(f32[2048,128]{1,0:T(8,128)S(1)} %bitcast_convert_fusion.5, f32[2048,8]{1,0:T(8,128)S(1)} %copy.43), kind=kLoop, calls=%fused_computation.23.clone.1 | loop fusion | flops 4194304 | bytes 5308416 | tf_op jit(solution)/shard_map/while/body/eval_jaxpr/convert_element_type | solution.py:83
  621.2 8.6 %multiply_convert_fusion.2 = bf16[2048,8,128]{2,1,0:T(8,128)(2,1)} fusion(f32[2048,128]{1,0:T(8,128)S(1)} %bitcast_convert_fusion.5, f32[2048,8]{1,0:T(8,128)S(1)} %copy.43), kind=kLoop, calls=%fused_computation.23.clone.1 | loop fusion | flops 4194304 | bytes 5308416 | tf_op jit(solution)/shard_map/while/body/eval_jaxpr/convert_element_type | solution.py:83
  637.3 8.6 %multiply_convert_fusion.2 = bf16[2048,8,128]{2,1,0:T(8,128)(2,1)} fusion(f32[2048,128]{1,0:T(8,128)S(1)} %bitcast_convert_fusion.5, f32[2048,8]{1,0:T(8,128)S(1)} %copy.43), kind=kLoop, calls=%fused_computation.23.clone.1 | loop fusion | flops 4194304 | bytes 5308416 | tf_op jit(solution)/shard_map/while/body/eval_jaxpr/convert_element_type | solution.py:83
  653.4 8.6 %multiply_convert_fusion.2 = bf16[2048,8,128]{2,1,0:T(8,128)(2,1)} fusion(f32[2048,128]{1,0:T(8,128)S(1)} %bitcast_convert_fusion.5, f32[2048,8]{1,0:T(8,128)S(1)} %copy.43), kind=kLoop, calls=%fused_computation.23.clone.1 | loop fusion | flops 4194304 | bytes 5308416 | tf_op jit(solution)/shard_map/while/body/eval_jaxpr/convert_element_type | solution.py:83
  685.6 8.6 %multiply_convert_fusion.2 = bf16[2048,8,128]{2,1,0:T(8,128)(2,1)} fusion(f32[2048,128]{1,0:T(8,128)S(1)} %bitcast_convert_fusion.5, f32[2048,8]{1,0:T(8,128)S(1)} %copy.43), kind=kLoop, calls=%fused_computation.23.clone.1 | loop fusion | flops 4194304 | bytes 5308416 | tf_op jit(solution)/shard_map/while/body/eval_jaxpr/convert_element_type | solution.py:83
  701.7 8.6 %multiply_convert_fusion.2 = bf16[2048,8,128]{2,1,0:T(8,128)(2,1)} fusion(f32[2048,128]{1,0:T(8,128)S(1)} %bitcast_convert_fusion.5, f32[2048,8]{1,0:T(8,128)S(1)} %copy.43), kind=kLoop, calls=%fused_computation.23.clone.1 | loop fusion | flops 4194304 | bytes 5308416 | tf_op jit(solution)/shard_map/while/body/eval_jaxpr/convert_element_type | solution.py:83
  717.8 8.6 %multiply_convert_fusion.2 = bf16[2048,8,128]{2,1,0:T(8,128)(2,1)} fusion(f32[2048,128]{1,0:T(8,128)S(1)} %bitcast_convert_fusion.5, f32[2048,8]{1,0:T(8,128)S(1)} %copy.43), kind=kLoop, calls=%fused_computation.23.clone.1 | loop fusion | flops 4194304 | bytes 5308416 | tf_op jit(solution)/shard_map/while/body/eval_jaxpr/convert_element_type | solution.py:83
  733.8 8.6 %multiply_convert_fusion.2 = bf16[2048,8,128]{2,1,0:T(8,128)(2,1)} fusion(f32[2048,128]{1,0:T(8,128)S(1)} %bitcast_convert_fusion.5, f32[2048,8]{1,0:T(8,128)S(1)} %copy.43), kind=kLoop, calls=%fused_computation.23.clone.1 | loop fusion | flops 4194304 | bytes 5308416 | tf_op jit(solution)/shard_map/while/body/eval_jaxpr/convert_element_type | solution.py:83
  750.1 48.0 %all-gather.11.cloned.1.call-done = bf16[2048,1024]{0,1:T(8,128)(2,1)} async-done(((bf16[256,1024]{0,1:T(8,128)(2,1)}), bf16[2048,1024]{0,1:T(8,128)(2,1)}) %all-gather.11.cloned.1.call-update) | async-done | bytes 4194320 | tf_op jit(solution)/shard_map/all_gather | solution.py:96
  798.1 48.4 %fusion.24 = f32[8,128,256]{2,0,1:T(8,128)S(1)} fusion(bf16[128,256,2048]{2,1,0:T(8,128)(2,1)} %bitcast.12, bf16[2048,8,128]{0,2,1:T(8,128)(2,1)} %bitcast.95, bf16[8,128,256]{2,1,0:T(8,128)(2,1)S(1)} %copy-done), kind=kOutput, calls=%fused_computation.36 | convolution fusion | flops 1074266112 | bytes 139984896 | tf_op jit(solution)/shard_map/wrc,csw->swr/dot_general | solution.py:99
  (261 shorter events, 240.6 us)
Async XLA Ops:
  6.5 27.4 %all-gather.7.cloned.1.call-start = ((), (), s32[]{:S(2)}) async-start(), calls=%async_computation.1 | async-start | bytes 1179648 | tf_op jit(solution)/shard_map/all_gather | solution.py:29
  7.3 50.2 %all-gather.5.cloned.1.call-start = ((), (), s32[]{:S(2)}) async-start(), calls=%async_computation | async-start | bytes 1179648 | tf_op jit(solution)/shard_map/all_gather | solution.py:30
  8.0 318.3 %all-gather.9.cloned.1.call-start = ((), (), s32[]{:S(2)}) async-start(), calls=%async_computation.2 | async-start | bytes 4718592 | tf_op jit(solution)/shard_map/all_gather | solution.py:58
  10.2 480.2 %all-reduce.2.cloned.1.call-start = ((), (), s32[]{:S(2)}) async-start(), calls=%async_computation.3 | async-start | bytes 2097152 | tf_op jit(solution)/shard_map/psum | solution.py:78
  438.2 360.0 %all-gather.11.cloned.1.call-start = ((), (), s32[]{:S(2)}) async-start(), calls=%async_computation.4 | async-start | bytes 4718592 | tf_op jit(solution)/shard_map/all_gather | solution.py:96
  490.4 307.7 %copy-start = (bf16[8,128,256]{2,1,0:T(8,128)(2,1)S(1)}, bf16[8,128,256]{2,1,0:T(8,128)(2,1)}, u32[]{:S(2)}) copy-start(bf16[8,128,256]{2,1,0:T(8,128)(2,1)} %param.13) | copy-start | bytes 1572868
Sparse Core Ops, SparseCore 0:
  8.9 24.9 all-gather.6
  35.5 21.8 all-gather.4
  59.0 47.4 all-gather.8
  438.3 52.0 all-reduce.1
  750.3 47.8 all-gather.10
where the time goes:
time: 859 us; the launch traced here: 854 us
  other arithmetic  423 us (49%)
  matrix products  209 us (24%)
  waiting for transfers between devices  144 us (17%)
  local copies, waits for them, and re-layouts  62.9 us (7%)
  between operations  13.2 us (2%)
    dynamic_update_slice x8, other arithmetic, shards(): lax.map(build, (split_waves(length), split_waves(amplitude_scale), split_...  232 us
    convert_element_type x16, other arithmetic, backward(): (weight.T[:, :, None] * psi.astype(jnp.float32)[:, None, :]).astype(jnp.b...  137 us
    dot_general x16, matrix products, backward(): lax.dot_general(onehot, terms, (((0,), (0,)), ((), ())), preferred_elemen...  82.3 us
    psum x1, waiting for transfers between devices, shards(): fields = lax.psum(partial_fields, 'wave')  51.6 us
    dot_general x1, matrix products, shards(): jnp.einsum('wrc,csw->swr', columns, piece.reshape(size, samples, waves),...  48.4 us
    all_gather x1, waiting for transfers between devices, shards(): piece = lax.all_gather(grad_rows, 'event', axis=0, tiled=True)  48 us
    dot_general x1, matrix products, shards(): jnp.einsum('wrc,swc->swr', columns, lax.all_gather(latent, 'event', axis=...  47.5 us
    dot_general x16, matrix products, forward(): jnp.dot(onehot, amp_rows, preferred_element_type=jnp.float32)  30.9 us
  transfers between devices with their start and end apart: 5, of which 4 were waited for; matrix products, arithmetic and copies ran while one was open for 32% of the time, Pallas kernels for 0%

commit v1 on v0

v1 whole, which is shorter than its diff:
```python
import functools
import math

import jax
import jax.numpy as jnp
from jax import lax
from jax.experimental import pallas as pl
from jax.experimental.pallas import tpu as pltpu
from jax.sharding import PartitionSpec as P

TILE = 256
LANES = 128
CHUNK = 512
GROUP = 16
NN = (((1,), (0,)), ((), ()))
NT = (((1,), (1,)), ((), ()))


def dot(a, b, dims):
    return lax.dot_general(a, b, dims, preferred_element_type=jnp.float32)


def spread_rows(dst, read, total):
    for k in range(total // LANES):
        row = read(k * LANES)
        dst[pl.ds(k * LANES, LANES), :] = jnp.broadcast_to(row, (LANES, LANES)).T


def gather_pieces(dst, src, pieces, width):
    for k in range(pieces):
        block, lane = (k * width) // TILE, (k * width) % TILE
        dst[block, :, lane : lane + width] = src(k)


def wide(column):
    return jnp.concatenate([column] * (TILE // LANES), axis=1)


def forward_kernel(pieces, width, coords, profile, latent, kern, amp, dist, col_l, col_g, prof, vec, acc):
    total = pieces * width
    blocks = total // TILE
    step = 64

    @pl.when(pl.program_id(0) == 0)
    def _():
        spread_rows(col_l, lambda k: coords[0:1, k : k + LANES], total)
        spread_rows(col_g, lambda k: coords[1:2, k : k + LANES], total)

        def over_i(i, t0):
            def over_j(j, t):
                col = pl.ds(pl.multiple_of(j * TILE, TILE), TILE)
                x_c, y_c = coords[0:1, col], coords[1:2, col]
                for r in range(0, TILE, step):
                    row = pl.ds(pl.multiple_of(i * TILE + r, step), step)
                    dx = wide(col_l[row, :]) - x_c
                    dy = wide(col_g[row, :]) - y_c
                    dist[t, r : r + step, :] = (dx * dx + dy * dy) * (-math.log2(math.e))
                return t + 1

            return lax.fori_loop(i, blocks, over_j, t0)

        lax.fori_loop(0, blocks, over_i, 0)

    gather_pieces(prof, lambda k: profile[k, 0], pieces, width)
    gather_pieces(vec, lambda k: latent[k, 0], pieces, width)
    per = TILE // LANES
    spread_rows(col_l, lambda k: prof[k // TILE, 0:1, k % TILE : k % TILE + LANES], total)
    spread_rows(col_g, lambda k: prof[k // TILE, 1:2, k % TILE : k % TILE + LANES], total)
    acc[...] = jnp.zeros_like(acc)

    def build(i, j, t):
        l_c, g_c = prof[j, 0:1, :], prof[j, 1:2, :]
        for r in range(0, TILE, step):
            row = pl.ds(pl.multiple_of(i * TILE + r, step), step)
            root = lax.rsqrt(wide(col_l[row, :]) + l_c)
            power = jnp.exp2(dist[t, r : r + step, :] * (root * root))
            scale = wide(col_g[row, :]) * g_c
            kern[0, t, r : r + step, :] = (scale * root * power).astype(jnp.bfloat16)

    def over_i(i, t0):
        build(i, i, t0)
        acc[i] += dot(vec[i], kern[0, t0], NN)

        def over_j(j, t):
            build(i, j, t)
            tile = kern[0, t]
            acc[j] += dot(vec[i], tile, NN)
            acc[i] += dot(vec[j], tile, NT)
            return t + 1

        return lax.fori_loop(i + 1, blocks, over_j, t0 + 1)

    lax.fori_loop(0, blocks, over_i, 0)
    for k in range(pieces):
        block, lane = (k * width) // TILE, (k * width) % TILE
        amp[k, 0] = acc[block, :, lane : lane + width].astype(amp.dtype)


def backward_kernel(pieces, width, kern, grad, out, vec, acc):
    total = pieces * width
    blocks = total // TILE
    gather_pieces(vec, lambda k: grad[k, 0], pieces, width)
    acc[...] = jnp.zeros_like(acc)

    def over_i(i, t0):
        acc[i] += dot(vec[i], kern[0, t0], NN)

        def over_j(j, t):
            tile = kern[0, t]
            acc[j] += dot(vec[i], tile, NN)
            acc[i] += dot(vec[j], tile, NT)
            return t + 1

        return lax.fori_loop(i + 1, blocks, over_j, t0 + 1)

    lax.fori_loop(0, blocks, over_i, 0)
    for k in range(pieces):
        block, lane = (k * width) // TILE, (k * width) % TILE
        out[k, 0] = acc[block, :, lane : lane + width].astype(out.dtype)


def field_kernel(samples, inner, first, last, rows, basis, label, field):
    span = GROUP * samples
    base = pl.program_id(0) * inner

    def one(c, _):
        at = pl.ds(pl.multiple_of(c * CHUNK, CHUNK), CHUNK)
        psi = basis[at, :]
        seg = jnp.broadcast_to(label[:, at], (samples, CHUNK))

        def over_g(g, total):
            part = rows[pl.ds(pl.multiple_of(g * span, span), span), :]
            full = dot(part, psi, NT)
            own = seg - g * GROUP
            for b in range(GROUP):
                total = total + jnp.where(own == b, full[b * samples : (b + 1) * samples, :], 0.0)
            return total

        start = jnp.zeros((samples, CHUNK), jnp.float32)
        field[:, at] = lax.fori_loop(first[base + c], last[base + c] + 1, over_g, start)
        return 0

    lax.fori_loop(0, inner, one, 0)


def sums_kernel(samples, inner, first, last, field, basis, label, sums):
    span = GROUP * samples
    base = pl.program_id(0) * inner

    @pl.when(pl.program_id(0) == 0)
    def _():
        sums[...] = jnp.zeros_like(sums)

    def one(c, _):
        at = pl.ds(pl.multiple_of(c * CHUNK, CHUNK), CHUNK)
        psi = basis[at, :]
        seg = jnp.broadcast_to(label[:, at], (samples, CHUNK))
        value = field[:, at]
        weight = -2.0 * value / (1.0 + value * value) / samples

        def over_g(g, _):
            own = seg - g * GROUP
            full = jnp.concatenate([jnp.where(own == b, weight, 0.0) for b in range(GROUP)], axis=0)
            high = full.astype(jnp.bfloat16)
            low = (full - high.astype(jnp.float32)).astype(jnp.bfloat16)
            at_g = pl.ds(pl.multiple_of(g * span, span), span)
            sums[at_g, :] += dot(high, psi, NN) + dot(low, psi, NN)
            return 0

        return lax.fori_loop(first[base + c], last[base + c] + 1, over_g, 0)

    lax.fori_loop(0, inner, one, 0)


def params(limit=60 << 20):
    return pltpu.CompilerParams(dimension_semantics=("arbitrary",), vmem_limit_bytes=limit)


def shards(count, latent, basis, event_bin, length, amplitude_scale, yield_norm, bin_coords):
    samples, waves, width = latent.shape
    total = bin_coords.shape[1]
    own = waves // count
    blocks = total // TILE
    tiles = blocks * (blocks + 1) // 2
    f32, bf16 = jnp.float32, jnp.bfloat16

    def exchange(values):
        return lax.all_to_all(values, "event", 0, 0)

    profile = jnp.stack(
        [length * length, amplitude_scale * jnp.sqrt(math.sqrt(2.0) * length)], axis=1
    ).reshape(count, own, 2, width)
    profile = exchange(profile)
    draws = exchange(jnp.transpose(latent, (1, 0, 2)).reshape(count, own, samples, width))

    piece = pl.BlockSpec((count, 1, samples, width), lambda w: (0, w, 0, 0))
    kern_spec = pl.BlockSpec((1, tiles, TILE, TILE), lambda w: (w, 0, 0, 0))
    kern, amp = pl.pallas_call(
        functools.partial(forward_kernel, count, width),
        out_shape=(
            jax.ShapeDtypeStruct((own, tiles, TILE, TILE), bf16),
            jax.ShapeDtypeStruct((count, own, samples, width), bf16),
        ),
        grid=(own,),
        in_specs=[
            pl.BlockSpec((2, total), lambda w: (0, 0)),
            pl.BlockSpec((count, 1, 2, width), lambda w: (0, w, 0, 0)),
            piece,
        ],
        out_specs=(kern_spec, piece),
        scratch_shapes=[
            pltpu.VMEM((tiles, TILE, TILE), f32),
            pltpu.VMEM((total, LANES), f32),
            pltpu.VMEM((total, LANES), f32),
            pltpu.VMEM((blocks, 2, TILE), f32),
            pltpu.VMEM((blocks, samples, TILE), bf16),
            pltpu.VMEM((blocks, samples, TILE), f32),
        ],
        compiler_params=params(),
        name="kern_forward",
    )(bin_coords, profile, draws)

    amp = exchange(amp).reshape(waves, samples, width)
    amp_rows = jnp.transpose(amp, (2, 1, 0)).reshape(width * samples, waves)

    events = basis.shape[0]
    block = min(events, 4096)
    inner = block // CHUNK
    grouped = event_bin.reshape(events // CHUNK, CHUNK) // GROUP
    first, last = grouped[:, 0], grouped[:, -1]
    basis_spec = pl.BlockSpec((block, waves), lambda e, *_: (e, 0))
    label_spec = pl.BlockSpec((1, block), lambda e, *_: (0, e))
    field_spec = pl.BlockSpec((samples, block), lambda e, *_: (0, e))
    rows_spec = pl.BlockSpec((width * samples, waves), lambda e, *_: (0, 0))
    field = pl.pallas_call(
        functools.partial(field_kernel, samples, inner),
        out_shape=jax.ShapeDtypeStruct((samples, events), f32),
        grid_spec=pltpu.PrefetchScalarGridSpec(
            num_scalar_prefetch=2,
            grid=(events // block,),
            in_specs=[rows_spec, basis_spec, label_spec],
            out_specs=field_spec,
        ),
        compiler_params=params(),
        name="event_field",
    )(first, last, amp_rows, basis, event_bin)
    field = lax.psum(field, "wave")
    sums = pl.pallas_call(
        functools.partial(sums_kernel, samples, inner),
        out_shape=jax.ShapeDtypeStruct((width * samples, waves), f32),
        grid_spec=pltpu.PrefetchScalarGridSpec(
            num_scalar_prefetch=2,
            grid=(events // block,),
            in_specs=[field_spec, basis_spec, label_spec],
            out_specs=rows_spec,
        ),
        compiler_params=params(),
        name="event_sums",
    )(first, last, field, basis, event_bin)

    sums = jnp.transpose(sums.reshape(width, samples, waves), (2, 1, 0))
    grad = (sums + 2.0 / samples * amp.astype(f32) * yield_norm[:, None, :]).astype(bf16)
    grad = exchange(grad.reshape(count, own, samples, width))
    pulled = pl.pallas_call(
        functools.partial(backward_kernel, count, width),
        out_shape=jax.ShapeDtypeStruct((count, own, samples, width), f32),
        grid=(own,),
        in_specs=[kern_spec, piece],
        out_specs=piece,
        scratch_shapes=[
            pltpu.VMEM((blocks, samples, TILE), bf16),
            pltpu.VMEM((blocks, samples, TILE), f32),
        ],
        compiler_params=params(),
        name="kern_backward",
    )(kern, grad)
    pulled = exchange(pulled).reshape(waves, samples, width)
    return jnp.transpose(pulled, (1, 0, 2)) + latent.astype(f32)


def solution(mesh):
    placed = (
        P(None, "wave", "event"),
        P("event", "wave"),
        P("event", None),
        P("wave", "event"),
        P("wave", "event"),
        P("wave", "event"),
        P(),
    )
    return jax.shard_map(
        functools.partial(shards, mesh.shape["event"]),
        mesh=mesh,
        in_specs=placed,
        out_specs=P(None, "wave", "event"),
        check_vma=False,
    )
```

time: 859 us -> 460 us (0.54)
  other arithmetic: 423 us -> 6.48 us
  Pallas kernels: 0 us -> 284 us
  matrix products: 209 us -> 0 us
  waiting for transfers between devices: 144 us -> 70.8 us
  blocking collectives: 0 us -> 68.3 us
  local copies, waits for them, and re-layouts: 62.9 us -> 6.02 us
  starting transfers between devices: 0.34 us -> 9.89 us
    pallas_call x0 -> x4, Pallas kernels: none -> 284 us  [the longest x1 135 us: shards(): pl.pallas_call(functools.partial(forward_kernel, count, width), out_shape...]
    dynamic_update_slice x8 -> x0, other arithmetic: 232 us -> none  [shards(): lax.map(build, (split_waves(length), split_waves(amplitude_scale), split_...]
    dot_general x34 -> x0, matrix products: 209 us -> none  [the longest x16 82.3 us: backward(): lax.dot_general(onehot, terms, (((0,), (0,)), ((), ())), preferred_elemen...]
    convert_element_type x49 -> x1, other arithmetic: 158 us -> 0.18 us  [shards(): (sums + 2.0 / samples * amp.astype(f32) * yield_norm[:, None, :]).astype(...]
    all_gather x4 -> x0, waiting for transfers between devices: 91.1 us -> none  [the longest x1 48 us: shards(): piece = lax.all_gather(grad_rows, 'event', axis=0, tiled=True)]
    all_to_all x0 -> x3, blocking collectives: none -> 68.3 us  [exchange(): return lax.all_to_all(values, 'event', 0, 0)]
    dynamic_slice x65 -> x0, local copies, waits for them, and re-layouts: 21.7 us -> none  [the longest x64 21 us: shards(): partial_fields = lax.map(forward, (basis_blocks, bin_blocks))]
    all_to_all x0 -> x2, waiting for transfers between devices: none -> 20.2 us  [exchange(): return lax.all_to_all(values, 'event', 0, 0)]
  transfers between devices with their start and end apart: 5 -> 3, of which waited for: 4 -> 3; matrix products, arithmetic and copies ran while one was open for 32% -> 1% of each run, Pallas kernels for 0% -> 0%
where the time goes in v1:
time: 460 us; the launch traced here: 459 us
  Pallas kernels  284 us (62%)
  waiting for transfers between devices  70.8 us (15%)
  blocking collectives  68.3 us (15%)
  between operations  13.5 us (3%)
  starting transfers between devices  9.89 us (2%)
  other arithmetic  6.48 us (1%)
  local copies, waits for them, and re-layouts  6.02 us (1%)
    pallas_call x1, Pallas kernels, shards(): pl.pallas_call(functools.partial(forward_kernel, count, width), out_shape...  135 us
    pallas_call x1, Pallas kernels, shards(): pl.pallas_call(functools.partial(backward_kernel, count, width), out_shap...  105 us
    all_to_all x3, blocking collectives, exchange(): return lax.all_to_all(values, 'event', 0, 0)  68.3 us
    psum x1, waiting for transfers between devices, shards(): field = lax.psum(field, 'wave')  50.6 us
    pallas_call x1, Pallas kernels, shards(): pl.pallas_call(functools.partial(sums_kernel, samples, inner), out_shape=...  24 us
    all_to_all x2, waiting for transfers between devices, exchange(): return lax.all_to_all(values, 'event', 0, 0)  20.2 us
    pallas_call x1, Pallas kernels, shards(): pl.pallas_call(functools.partial(field_kernel, samples, inner), out_shape...  19.3 us
    all_to_all x2, starting transfers between devices, exchange(): return lax.all_to_all(values, 'event', 0, 0)  9.85 us
  transfers between devices with their start and end apart: 3, of which 3 were waited for; matrix products, arithmetic and copies ran while one was open for 1% of the time, Pallas kernels for 0%

profile of v1, /device:TPU:0, one launch (start us, length us, event | category | flops | bytes accessed | tf_op | source)
XLA Modules:
  0.0 458.8 jit_solution(1648929297529793859)
XLA Ops:
  6.5 1.1 sqrt_multiply_fusion
  7.6 0.1 stack.10
  7.8 0.1 stack.9
  7.9 0.9 pad_maximum_fusion
  8.8 6.4 %all-to-all-start = ((f32[8,16,2,256]{3,2,1,0:T(2,128)}), f32[8,16,2,256]{3,2,1,0:T(2,128)S(1)}, u32[]{:S(2)}, u32[]{:S(2)}) async-start(f32[8,16,2,256]{3,2,1,0:T(2,128)} %pad_maximum_fusion), calls=%async_computation | async-start | bytes 524288 | tf_op jit(solution)/shard_map/all_to_all | solution.py:188
  15.2 1.3 copy.8
  16.5 8.4 %all-to-all-done.profile = f32[8,16,2,256]{3,2,1,0:T(2,128)S(1)} async-done(((f32[8,16,2,256]{3,2,1,0:T(2,128)}), f32[8,16,2,256]{3,2,1,0:T(2,128)S(1)}, u32[]{:S(2)}, u32[]{:S(2)}) %all-to-all-start) | async-done | bytes 262176 | tf_op jit(solution)/shard_map/all_to_all | solution.py:188
  24.9 0.0 copy-start.1
  24.9 18.4 %all_to_all.25.latent = bf16[8,16,8,256]{3,2,1,0:T(8,128)(2,1)} all-to-all(bf16[8,16,8,256]{3,2,1,0:T(8,128)(2,1)S(1)} %bitcast.25), channel_id=1, replica_groups=mesh['wave'=4,'event'=8] {'event'}, dimensions={0} | all-to-all | bytes 1048576 | tf_op jit(solution)/shard_map/all_to_all | solution.py:188
  43.3 0.0 copy-done.1
  43.3 135.3 %kern_forward.1 = (bf16[16,36,256,256]{3,2,1,0:T(8,128)(2,1)}, bf16[8,16,8,256]{3,2,1,0:T(8,128)(2,1)}) custom-call(f32[2,2048]{1,0:T(2,128)} %coords.1, f32[8,16,2,256]{3,2,1,0:T(2,128)} %copy-done.1, bf16[8,16,8,256]{3,2,1,0:T(8,128)(2,1)} %all_to_all.25.latent), custom_call_target="tpu_custom_call" | custom-call | tf_op jit(solution)/shard_map/kern_forward/pallas_call | solution.py:198
  178.6 3.5 all-to-all-start.2
  182.1 0.0 all-reduce.2.cloned.1.call-start
  182.1 0.6 broadcast.14
  182.7 1.9 reduce.3
  184.7 0.1 copy.9
  184.8 0.1 add_select_fusion
  185.0 0.6 slice_bitcast_fusion
  185.6 11.8 %all-to-all-done.2 = bf16[8,16,8,256]{3,2,1,0:T(8,128)(2,1)S(1)} async-done(((bf16[8,16,8,256]{3,2,1,0:T(8,128)(2,1)}), bf16[8,16,8,256]{3,2,1,0:T(8,128)(2,1)S(1)}, u32[]{:S(2)}, u32[]{:S(2)}) %all-to-all-start.2) | async-done | bytes 524320 | tf_op jit(solution)/shard_map/all_to_all | solution.py:188
  197.3 1.4 copy.13
  198.7 19.3 %event_field.1 = f32[8,32768]{1,0:T(8,128)} custom-call(s32[64]{0:T(128)} %get-tuple-element.10.first, s32[64]{0:T(128)} %get-tuple-element.9.last, bf16[2048,128]{1,0:T(8,128)(2,1)} %bitcast.26, bf16[32768,128]{1,0:T(8,128)(2,1)} %basis.3, s32[1,32768]{1,0:T(1,128)} %label.3), custom_call_target="tpu_custom_call" | custom-call | tf_op jit(solution)/shard_map/event_field/pallas_call | solution.py:235
  218.0 0.0 all-reduce.2.cloned.1.call-update
  218.0 0.9 broadcast_multiply_fusion
  218.9 50.6 %all-reduce.2.cloned.1.call-done.field = f32[8,32768]{1,0:T(8,128)} async-done(((f32[8,32768]{1,0:T(8,128)}), f32[8,32768]{1,0:T(8,128)}) %all-reduce.2.cloned.1.call-update) | async-done | bytes 1048592 | tf_op jit(solution)/shard_map/psum | solution.py:247
  269.6 24.0 %event_sums.1 = f32[2048,128]{1,0:T(8,128)} custom-call(s32[64]{0:T(128)} %get-tuple-element.10.first, s32[64]{0:T(128)} %get-tuple-element.9.last, f32[8,32768]{1,0:T(8,128)} %all-reduce.2.cloned.1.call-done.field, bf16[32768,128]{1,0:T(8,128)(2,1)} %basis.3, s32[1,32768]{1,0:T(1,128)} %label.3), custom_call_target="tpu_custom_call" | custom-call | tf_op jit(solution)/shard_map/event_sums/pallas_call | solution.py:248
  293.5 1.7 copy.14
  295.3 0.2 fusion
  295.4 19.8 %all_to_all.26.grad = bf16[8,16,8,256]{3,2,1,0:T(8,128)(2,1)} all-to-all(bf16[8,16,8,256]{3,2,1,0:T(8,128)(2,1)S(1)} %bitcast.24), channel_id=1, replica_groups=mesh['wave'=4,'event'=8] {'event'}, dimensions={0} | all-to-all | bytes 1048576 | tf_op jit(solution)/shard_map/all_to_all | solution.py:188
  315.3 105.4 %kern_backward.1 = f32[8,16,8,256]{3,2,1,0:T(8,128)} custom-call(bf16[16,36,256,256]{3,2,1,0:T(8,128)(2,1)} %get-tuple-element.7.kern, bf16[8,16,8,256]{3,2,1,0:T(8,128)(2,1)} %all_to_all.26.grad), custom_call_target="tpu_custom_call" | custom-call | tf_op jit(solution)/shard_map/kern_backward/pallas_call | solution.py:264
  420.6 30.0 %all_to_all.27 = f32[8,16,8,256]{3,2,1,0:T(8,128)S(1)} all-to-all(f32[8,16,8,256]{3,2,1,0:T(8,128)} %kern_backward.1), channel_id=1, replica_groups=mesh['wave'=4,'event'=8] {'event'}, dimensions={0} | all-to-all | bytes 2097152 | tf_op jit(solution)/shard_map/all_to_all | solution.py:188
  450.7 0.0 copy-done
  450.7 1.3 bitcast_add_fusion
  (2 shorter events, 0.0 us)
Async XLA Ops:
  6.5 444.1 %copy-start = (bf16[8,128,256]{2,1,0:T(8,128)(2,1)S(1)}, bf16[8,128,256]{2,1,0:T(8,128)(2,1)}, u32[]{:S(2)}) copy-start(bf16[8,128,256]{2,1,0:T(8,128)(2,1)} %param.7) | copy-start | bytes 1572868
  8.8 16.1 %all-to-all-start = ((f32[8,16,2,256]{3,2,1,0:T(2,128)}), f32[8,16,2,256]{3,2,1,0:T(2,128)S(1)}, u32[]{:S(2)}, u32[]{:S(2)}) async-start(f32[8,16,2,256]{3,2,1,0:T(2,128)} %pad_maximum_fusion), calls=%async_computation | async-start | bytes 524288 | tf_op jit(solution)/shard_map/all_to_all | solution.py:188
  24.9 18.4 %copy-start.1 = (f32[8,16,2,256]{3,2,1,0:T(2,128)}, f32[8,16,2,256]{3,2,1,0:T(2,128)S(1)}, u32[]{:S(2)}) copy-start(f32[8,16,2,256]{3,2,1,0:T(2,128)S(1)} %all-to-all-done.profile) | copy-start | bytes 786436
  178.6 18.8 %all-to-all-start.2 = ((bf16[8,16,8,256]{3,2,1,0:T(8,128)(2,1)}), bf16[8,16,8,256]{3,2,1,0:T(8,128)(2,1)S(1)}, u32[]{:S(2)}, u32[]{:S(2)}) async-start(bf16[8,16,8,256]{3,2,1,0:T(8,128)(2,1)} %get-tuple-element.8), calls=%async_computation.2 | async-start | bytes 1048576 | tf_op jit(solution)/shard_map/all_to_all | solution.py:188
  182.1 87.5 %all-reduce.2.cloned.1.call-start = ((), (), s32[]{:S(2)}) async-start(), calls=%async_computation.5 | async-start | bytes 2097152 | tf_op jit(solution)/shard_map/psum | solution.py:247
Sparse Core Ops, SparseCore 0:
  218.1 51.3 all-reduce.1

commit v2 on v1

v2 whole, which is shorter than its diff:
```python
import functools
import math

import jax
import jax.numpy as jnp
from jax import lax
from jax.experimental import pallas as pl
from jax.experimental.pallas import tpu as pltpu
from jax.sharding import PartitionSpec as P

TILE = 256
LANES = 128
CHUNK = 1024
GROUP = 16
MESH = pl.DeviceIdType.MESH
NN = (((1,), (0,)), ((), ()))
NT = (((1,), (1,)), ((), ()))


def dot(a, b, dims):
    return lax.dot_general(a, b, dims, preferred_element_type=jnp.float32)


def spread_rows(dst, read, total):
    for k in range(total // LANES):
        row = read(k * LANES)
        dst[pl.ds(k * LANES, LANES), :] = jnp.broadcast_to(row, (LANES, LANES)).T


def gather_pieces(dst, src, pieces, width):
    for k in range(pieces):
        block, lane = (k * width) // TILE, (k * width) % TILE
        dst[block, :, lane : lane + width] = src(k)


def wide(column):
    return jnp.concatenate([column] * (TILE // LANES), axis=1)


def tile_pairs(blocks):
    return [(i, j) for i in range(blocks) for j in range(i, blocks)]


def add(held, term):
    return term if held is None else held + term


def multiply(sums, vec, tile, i, j):
    sums[j] = add(sums[j], dot(vec[i], tile, NN))
    if j > i:
        sums[i] = add(sums[i], dot(vec[j], tile, NT))


def scatter_pieces(dst, sums, pieces, width):
    for k in range(pieces):
        block, lane = (k * width) // TILE, (k * width) % TILE
        dst[k, 0] = sums[block][:, lane : lane + width].astype(dst.dtype)


def forward_kernel(pieces, width, coords, profile, latent, kern, amp, dist, col_l, col_g, prof, vec):
    total = pieces * width
    pairs = tile_pairs(total // TILE)
    step = 64

    @pl.when(pl.program_id(0) == 0)
    def _():
        spread_rows(col_l, lambda k: coords[0:1, k : k + LANES], total)
        spread_rows(col_g, lambda k: coords[1:2, k : k + LANES], total)

        def over_i(i, t0):
            def over_j(j, t):
                col = pl.ds(pl.multiple_of(j * TILE, TILE), TILE)
                x_c, y_c = coords[0:1, col], coords[1:2, col]
                for r in range(0, TILE, step):
                    row = pl.ds(pl.multiple_of(i * TILE + r, step), step)
                    dx = wide(col_l[row, :]) - x_c
                    dy = wide(col_g[row, :]) - y_c
                    dist[t, r : r + step, :] = (dx * dx + dy * dy) * (-math.log2(math.e))
                return t + 1

            return lax.fori_loop(i, total // TILE, over_j, t0)

        lax.fori_loop(0, total // TILE, over_i, 0)

    gather_pieces(prof, lambda k: profile[k, 0], pieces, width)
    gather_pieces(vec, lambda k: latent[k, 0], pieces, width)
    spread_rows(col_l, lambda k: prof[k // TILE, 0:1, k % TILE : k % TILE + LANES], total)
    spread_rows(col_g, lambda k: prof[k // TILE, 1:2, k % TILE : k % TILE + LANES], total)

    sums = [None] * (total // TILE)
    for t, (i, j) in enumerate(pairs):
        l_c, g_c = prof[j, 0:1, :], prof[j, 1:2, :]
        strips = []
        for r in range(0, TILE, step):
            row = pl.ds(i * TILE + r, step)
            root = lax.rsqrt(wide(col_l[row, :]) + l_c)
            power = jnp.exp2(dist[t, r : r + step, :] * (root * root))
            scale = wide(col_g[row, :]) * g_c
            strip = (scale * root * power).astype(jnp.bfloat16)
            kern[0, t, r : r + step, :] = strip
            strips.append(strip)
        multiply(sums, vec, jnp.concatenate(strips, axis=0), i, j)
    scatter_pieces(amp, sums, pieces, width)


def backward_kernel(pieces, width, kern, grad, out, vec):
    total = pieces * width
    gather_pieces(vec, lambda k: grad[k, 0], pieces, width)
    sums = [None] * (total // TILE)
    for t, (i, j) in enumerate(tile_pairs(total // TILE)):
        multiply(sums, vec, kern[0, t], i, j)
    scatter_pieces(out, sums, pieces, width)


def field_kernel(samples, inner, first, last, rows, basis, label, field):
    span = GROUP * samples
    base = pl.program_id(0) * inner

    def one(c, _):
        at = pl.ds(pl.multiple_of(c * CHUNK, CHUNK), CHUNK)
        psi = basis[at, :]
        seg = jnp.broadcast_to(label[:, at], (samples, CHUNK))

        def over_g(g, total):
            part = rows[pl.ds(pl.multiple_of(g * span, span), span), :]
            full = dot(part, psi, NT)
            own = seg - g * GROUP
            for b in range(GROUP):
                total = total + jnp.where(own == b, full[b * samples : (b + 1) * samples, :], 0.0)
            return total

        start = jnp.zeros((samples, CHUNK), jnp.float32)
        total = lax.fori_loop(first[base + c], last[base + c] + 1, over_g, start)
        field[0, :, at] = total.astype(field.dtype)
        return 0

    lax.fori_loop(0, inner, one, 0)


def sums_kernel(samples, inner, first, last, weight, basis, label, sums):
    span = GROUP * samples
    base = pl.program_id(0) * inner

    @pl.when(pl.program_id(0) == 0)
    def _():
        sums[...] = jnp.zeros_like(sums)

    def one(c, _):
        at = pl.ds(pl.multiple_of(c * CHUNK, CHUNK), CHUNK)
        psi = basis[at, :]
        seg = jnp.broadcast_to(label[:, at], (samples, CHUNK))
        value = weight[0, :, at].astype(jnp.float32)

        def over_g(g, _):
            own = seg - g * GROUP
            full = jnp.concatenate([jnp.where(own == b, value, 0.0) for b in range(GROUP)], axis=0)
            at_g = pl.ds(pl.multiple_of(g * span, span), span)
            sums[at_g, :] += dot(full.astype(jnp.bfloat16), psi, NN)
            return 0

        return lax.fori_loop(first[base + c], last[base + c] + 1, over_g, 0)

    lax.fori_loop(0, inner, one, 0)


def greet(axis, count):
    me = lax.axis_index(axis)
    peers = [lax.rem(me + d, count) for d in range(1, count)]
    barrier = pltpu.get_barrier_semaphore()
    for peer in peers:
        pl.semaphore_signal(barrier, inc=1, device_id={axis: peer}, device_id_type=MESH)
    pl.semaphore_wait(barrier, count - 1)
    return me, peers


def exchange_kernel(axis, count, arrays, *refs):
    sources, targets = refs[:arrays], refs[arrays : 2 * arrays]
    send, recv = refs[2 * arrays :]
    me, peers = greet(axis, count)
    copies = []
    for a in range(arrays):
        for d, peer in enumerate(peers):
            copy = pltpu.make_async_remote_copy(
                src_ref=sources[a].at[peer],
                dst_ref=targets[a].at[me],
                send_sem=send.at[a, d],
                recv_sem=recv.at[a, d],
                device_id={axis: peer},
                device_id_type=MESH,
            )
            copy.start()
            copies.append(copy)
    for a in range(arrays):
        targets[a][me] = sources[a][me]
    for copy in copies:
        copy.wait()


def exchange(axis, count, ident, *values):
    vmem = pl.BlockSpec(memory_space=pltpu.VMEM)
    arrays = len(values)
    return pl.pallas_call(
        functools.partial(exchange_kernel, axis, count, arrays),
        out_shape=[jax.ShapeDtypeStruct(v.shape, v.dtype) for v in values],
        in_specs=[vmem] * arrays,
        out_specs=[vmem] * arrays,
        scratch_shapes=[pltpu.SemaphoreType.DMA((arrays, count - 1))] * 2,
        compiler_params=pltpu.CompilerParams(
            collective_id=ident, has_side_effects=True, vmem_limit_bytes=8 << 20
        ),
        name=f"exchange_{ident}",
    )(*values)


def weight_kernel(axis, count, samples, partial, weight, landed, made, send, recv, local):
    me, peers = greet(axis, count)
    copies = []
    for d, peer in enumerate(peers):
        copy = pltpu.make_async_remote_copy(
            src_ref=partial.at[peer],
            dst_ref=landed.at[d],
            send_sem=send.at[0, d],
            recv_sem=recv.at[0, d],
            device_id={axis: peer},
            device_id_type=MESH,
        )
        copy.start()
        copies.append(copy)
    for copy in copies:
        copy.wait()
    total = partial[me].astype(jnp.float32)
    for d in range(count - 1):
        total = total + landed[d].astype(jnp.float32)
    made[...] = (-2.0 * total / (1.0 + total * total) / samples).astype(made.dtype)
    keep = pltpu.make_async_copy(made, weight.at[me], local)
    keep.start()
    keep.wait()
    copies = []
    for d, peer in enumerate(peers):
        copy = pltpu.make_async_remote_copy(
            src_ref=weight.at[me],
            dst_ref=weight.at[me],
            send_sem=send.at[1, d],
            recv_sem=recv.at[1, d],
            device_id={axis: peer},
            device_id_type=MESH,
        )
        copy.start()
        copies.append(copy)
    for copy in copies:
        copy.wait()


def share_weight(axis, count, ident, samples, partial):
    vmem = pl.BlockSpec(memory_space=pltpu.VMEM)
    shape, dtype = partial.shape, partial.dtype
    return pl.pallas_call(
        functools.partial(weight_kernel, axis, count, samples),
        out_shape=jax.ShapeDtypeStruct(shape, dtype),
        in_specs=[vmem],
        out_specs=vmem,
        scratch_shapes=[
            pltpu.VMEM((count - 1,) + shape[1:], dtype),
            pltpu.VMEM(shape[1:], dtype),
            pltpu.SemaphoreType.DMA((2, count - 1)),
            pltpu.SemaphoreType.DMA((2, count - 1)),
            pltpu.SemaphoreType.DMA,
        ],
        compiler_params=pltpu.CompilerParams(
            collective_id=ident, has_side_effects=True, vmem_limit_bytes=12 << 20
        ),
        name="share_weight",
    )(partial)


def params(limit=60 << 20):
    return pltpu.CompilerParams(dimension_semantics=("arbitrary",), vmem_limit_bytes=limit)


def shards(count, splits, latent, basis, event_bin, length, amplitude_scale, yield_norm, bin_coords):
    samples, waves, width = latent.shape
    total = bin_coords.shape[1]
    own = waves // count
    blocks = total // TILE
    tiles = blocks * (blocks + 1) // 2
    f32, bf16 = jnp.float32, jnp.bfloat16

    profile = jnp.stack(
        [length * length, amplitude_scale * jnp.sqrt(math.sqrt(2.0) * length)], axis=1
    ).reshape(count, own, 2, width)
    draws = jnp.transpose(latent, (1, 0, 2)).reshape(count, own, samples, width)
    profile, draws = exchange("event", count, 0, profile, draws)

    piece = pl.BlockSpec((count, 1, samples, width), lambda w: (0, w, 0, 0))
    kern_spec = pl.BlockSpec((1, tiles, TILE, TILE), lambda w: (w, 0, 0, 0))
    kern, amp = pl.pallas_call(
        functools.partial(forward_kernel, count, width),
        out_shape=(
            jax.ShapeDtypeStruct((own, tiles, TILE, TILE), bf16),
            jax.ShapeDtypeStruct((count, own, samples, width), bf16),
        ),
        grid=(own,),
        in_specs=[
            pl.BlockSpec((2, total), lambda w: (0, 0)),
            pl.BlockSpec((count, 1, 2, width), lambda w: (0, w, 0, 0)),
            piece,
        ],
        out_specs=(kern_spec, piece),
        scratch_shapes=[
            pltpu.VMEM((tiles, TILE, TILE), f32),
            pltpu.VMEM((total, LANES), f32),
            pltpu.VMEM((total, LANES), f32),
            pltpu.VMEM((blocks, 2, TILE), f32),
            pltpu.VMEM((blocks, samples, TILE), bf16),
        ],
        compiler_params=params(),
        name="kern_forward",
    )(bin_coords, profile, draws)

    (amp,) = exchange("event", count, 1, amp)
    amp = amp.reshape(waves, samples, width)
    amp_rows = jnp.transpose(amp, (2, 1, 0)).reshape(width * samples, waves)

    events = basis.shape[0]
    block = min(events // splits, 4096)
    per = events // splits // block
    inner = block // CHUNK
    grouped = event_bin.reshape(events // CHUNK, CHUNK) // GROUP
    first, last = grouped[:, 0], grouped[:, -1]
    basis_spec = pl.BlockSpec((block, waves), lambda e, *_: (e, 0))
    label_spec = pl.BlockSpec((1, block), lambda e, *_: (0, e))
    field_spec = pl.BlockSpec((1, samples, block), lambda e, *_: (e // per, 0, e % per))
    rows_spec = pl.BlockSpec((width * samples, waves), lambda e, *_: (0, 0))
    field = pl.pallas_call(
        functools.partial(field_kernel, samples, inner),
        out_shape=jax.ShapeDtypeStruct((splits, samples, events // splits), bf16),
        grid_spec=pltpu.PrefetchScalarGridSpec(
            num_scalar_prefetch=2,
            grid=(events // block,),
            in_specs=[rows_spec, basis_spec, label_spec],
            out_specs=field_spec,
        ),
        compiler_params=params(),
        name="event_field",
    )(first, last, amp_rows, basis, event_bin)
    weight = share_weight("wave", splits, 2, samples, field)
    sums = pl.pallas_call(
        functools.partial(sums_kernel, samples, inner),
        out_shape=jax.ShapeDtypeStruct((width * samples, waves), f32),
        grid_spec=pltpu.PrefetchScalarGridSpec(
            num_scalar_prefetch=2,
            grid=(events // block,),
            in_specs=[field_spec, basis_spec, label_spec],
            out_specs=rows_spec,
        ),
        compiler_params=params(),
        name="event_sums",
    )(first, last, weight, basis, event_bin)

    sums = jnp.transpose(sums.reshape(width, samples, waves), (2, 1, 0))
    grad = (sums + 2.0 / samples * amp.astype(f32) * yield_norm[:, None, :]).astype(bf16)
    (grad,) = exchange("event", count, 3, grad.reshape(count, own, samples, width))
    pulled = pl.pallas_call(
        functools.partial(backward_kernel, count, width),
        out_shape=jax.ShapeDtypeStruct((count, own, samples, width), bf16),
        grid=(own,),
        in_specs=[kern_spec, piece],
        out_specs=piece,
        scratch_shapes=[
            pltpu.VMEM((blocks, samples, TILE), bf16),
        ],
        compiler_params=params(),
        name="kern_backward",
    )(kern, grad)
    (pulled,) = exchange("event", count, 4, pulled)
    pulled = pulled.reshape(waves, samples, width).astype(f32)
    return jnp.transpose(pulled, (1, 0, 2)) + latent.astype(f32)


def solution(mesh):
    placed = (
        P(None, "wave", "event"),
        P("event", "wave"),
        P("event", None),
        P("wave", "event"),
        P("wave", "event"),
        P("wave", "event"),
        P(),
    )
    return jax.shard_map(
        functools.partial(shards, mesh.shape["event"], mesh.shape["wave"]),
        mesh=mesh,
        in_specs=placed,
        out_specs=P(None, "wave", "event"),
        check_vma=False,
    )
```

time: 460 us -> 225 us (0.49)
  Pallas kernels: 284 us -> 205 us
  waiting for transfers between devices: 70.8 us -> 0 us
  blocking collectives: 68.3 us -> 0 us
  between operations: 13.5 us -> 0.16 us
  starting transfers between devices: 9.89 us -> 0 us
  local copies, waits for them, and re-layouts: 6.02 us -> 12.2 us
    pallas_call x0 -> x5, Pallas kernels: none -> 82.1 us  [the longest x4 63.8 us: exchange(): pl.pallas_call(functools.partial(exchange_kernel, axis, count, arrays), o...]
    pallas_call x1, Pallas kernels: 135 us -> 57 us  [shards(): pl.pallas_call(functools.partial(forward_kernel, count, width), out_shape...]
    pallas_call x1, Pallas kernels: 105 us -> 35.5 us  [shards(): pl.pallas_call(functools.partial(backward_kernel, count, width), out_shap...]
    all_to_all x3 -> x0, blocking collectives: 68.3 us -> none  [exchange(): return lax.all_to_all(values, 'event', 0, 0)]
    psum x1 -> x0, waiting for transfers between devices: 50.6 us -> none  [shards(): field = lax.psum(field, 'wave')]
    all_to_all x2 -> x0, waiting for transfers between devices: 20.2 us -> none  [exchange(): return lax.all_to_all(values, 'event', 0, 0)]
    all_to_all x2 -> x0, starting transfers between devices: 9.85 us -> none  [exchange(): return lax.all_to_all(values, 'event', 0, 0)]
    pallas_call x1, Pallas kernels: 24 us -> 14.9 us  [shards(): pl.pallas_call(functools.partial(sums_kernel, samples, inner), out_shape=...]
  transfers between devices with their start and end apart: 3 -> 0, of which waited for: 3 -> 0; matrix products, arithmetic and copies ran while one was open for 1% -> 0% of each run, Pallas kernels for 0% -> 0%
where the time goes in v2:
time: 225 us; the launch traced here: 223 us
  Pallas kernels  205 us (91%)
  local copies, waits for them, and re-layouts  12.2 us (5%)
  other arithmetic  5.99 us (3%)
    pallas_call x4, Pallas kernels, exchange(): pl.pallas_call(functools.partial(exchange_kernel, axis, count, arrays), o...  63.8 us
    pallas_call x1, Pallas kernels, shards(): pl.pallas_call(functools.partial(forward_kernel, count, width), out_shape...  57 us
    pallas_call x1, Pallas kernels, shards(): pl.pallas_call(functools.partial(backward_kernel, count, width), out_shap...  35.5 us
    pallas_call x1, Pallas kernels, share_weight(): pl.pallas_call(functools.partial(weight_kernel, axis, count, samples), ou...  18.4 us
    pallas_call x1, Pallas kernels, shards(): pl.pallas_call(functools.partial(field_kernel, samples, inner), out_shape...  15.3 us
    pallas_call x1, Pallas kernels, shards(): pl.pallas_call(functools.partial(sums_kernel, samples, inner), out_shape=...  14.9 us
    unnamed x17, local copies, waits for them, and re-layouts  6.75 us

profile of v2, /device:TPU:0, one launch (start us, length us, event | category | flops | bytes accessed | tf_op | source)
XLA Modules:
  0.0 223.2 jit_solution(17773614783113488972)
XLA Ops:
  0.0 1.1 sqrt_multiply_fusion
  1.1 0.1 stack.10
  1.2 0.1 stack.9
  1.4 0.2 pad_maximum_fusion.refs_0_
  1.6 1.3 copy.8
  2.9 19.5 %exchange_0.1 = (f32[8,16,2,256]{3,2,1,0:T(2,128)S(1)}, bf16[8,16,8,256]{3,2,1,0:T(8,128)(2,1)S(1)}) custom-call(f32[8,16,2,256]{3,2,1,0:T(2,128)S(1)} %pad_maximum_fusion.refs_0_, bf16[8,16,8,256]{3,2,1,0:T(8,128)(2,1)S(1)} %bitcast.24), custom_call_target="tpu_custom_call" | custom-call | tf_op jit(solution)/shard_map/exchange_0/pallas_call | solution.py:202
  22.5 0.8 copy-done.5
  23.2 0.7 copy-done.6
  24.0 57.0 %kern_forward.1 = (bf16[16,36,256,256]{3,2,1,0:T(8,128)(2,1)}, bf16[8,16,8,256]{3,2,1,0:T(8,128)(2,1)}) custom-call(f32[2,2048]{1,0:T(2,128)} %coords.1, f32[8,16,2,256]{3,2,1,0:T(2,128)} %copy-done.6, bf16[8,16,8,256]{3,2,1,0:T(8,128)(2,1)} %copy-done.5), custom_call_target="tpu_custom_call" | custom-call | tf_op jit(solution)/shard_map/kern_forward/pallas_call | solution.py:296
  81.0 0.5 broadcast.14
  81.5 1.9 reduce.3
  83.4 0.2 copy.9
  83.6 0.3 add_select_fusion
  83.9 0.6 slice_bitcast_fusion
  84.5 1.0 copy-done.4
  85.5 15.2 %exchange_1.1 = bf16[8,16,8,256]{3,2,1,0:T(8,128)(2,1)S(1)} custom-call(bf16[8,16,8,256]{3,2,1,0:T(8,128)(2,1)S(1)} %copy-done.4), custom_call_target="tpu_custom_call" | custom-call | tf_op jit(solution)/shard_map/exchange_1/pallas_call | solution.py:202
  100.7 1.3 copy.13
  102.1 15.3 %event_field.1.partial = bf16[4,8,8192]{2,1,0:T(8,128)(2,1)} custom-call(s32[32]{0:T(128)} %get-tuple-element.14.first, s32[32]{0:T(128)} %get-tuple-element.13.last, bf16[2048,128]{1,0:T(8,128)(2,1)} %bitcast.27, bf16[32768,128]{1,0:T(8,128)(2,1)} %basis.3, s32[1,32768]{1,0:T(1,128)} %label.3), custom_call_target="tpu_custom_call" | custom-call | tf_op jit(solution)/shard_map/event_field/pallas_call | solution.py:334
  117.4 1.0 copy-done.2
  118.4 18.4 %share_weight.1.weight = bf16[4,8,8192]{2,1,0:T(8,128)(2,1)S(1)} custom-call(bf16[4,8,8192]{2,1,0:T(8,128)(2,1)S(1)} %copy-done.2), custom_call_target="tpu_custom_call" | custom-call | tf_op jit(solution)/shard_map/share_weight/pallas_call | solution.py:257
  136.8 0.8 copy-done.3
  137.6 14.9 %event_sums.1 = f32[2048,128]{1,0:T(8,128)} custom-call(s32[32]{0:T(128)} %get-tuple-element.14.first, s32[32]{0:T(128)} %get-tuple-element.13.last, bf16[4,8,8192]{2,1,0:T(8,128)(2,1)} %copy-done.3, bf16[32768,128]{1,0:T(8,128)(2,1)} %basis.3, s32[1,32768]{1,0:T(1,128)} %label.3), custom_call_target="tpu_custom_call" | custom-call | tf_op jit(solution)/shard_map/event_sums/pallas_call | solution.py:347
  152.6 1.7 copy.14
  154.3 0.9 broadcast_multiply_fusion
  155.2 0.2 fusion
  155.4 14.4 %exchange_3.1.grad = bf16[8,16,8,256]{3,2,1,0:T(8,128)(2,1)S(1)} custom-call(bf16[8,16,8,256]{3,2,1,0:T(8,128)(2,1)S(1)} %bitcast.23), custom_call_target="tpu_custom_call" | custom-call | tf_op jit(solution)/shard_map/exchange_3/pallas_call | solution.py:202
  169.8 0.8 copy-done
  170.6 35.5 %kern_backward.1.refs_0_ = bf16[8,16,8,256]{3,2,1,0:T(8,128)(2,1)} custom-call(bf16[16,36,256,256]{3,2,1,0:T(8,128)(2,1)} %get-tuple-element.11.kern, bf16[8,16,8,256]{3,2,1,0:T(8,128)(2,1)} %copy-done), custom_call_target="tpu_custom_call" | custom-call | tf_op jit(solution)/shard_map/kern_backward/pallas_call | solution.py:363
  206.1 1.0 copy-done.1
  207.1 14.7 %exchange_4.1 = bf16[8,16,8,256]{3,2,1,0:T(8,128)(2,1)S(1)} custom-call(bf16[8,16,8,256]{3,2,1,0:T(8,128)(2,1)S(1)} %copy-done.1), custom_call_target="tpu_custom_call" | custom-call | tf_op jit(solution)/shard_map/exchange_4/pallas_call | solution.py:202
  221.8 0.1 bitcast_convert_fusion
  221.9 1.3 bitcast_add_fusion
  (10 shorter events, 0.0 us)
Async XLA Ops:
  0.0 221.9 %copy-start.7 = (bf16[8,128,256]{2,1,0:T(8,128)(2,1)S(1)}, bf16[8,128,256]{2,1,0:T(8,128)(2,1)}, u32[]{:S(2)}) copy-start(bf16[8,128,256]{2,1,0:T(8,128)(2,1)} %param.7) | copy-start | bytes 1572868
  22.4 0.8 copy-start.5
  23.2 0.7 copy-start.6
  84.5 1.0 copy-start.4
  117.3 1.0 copy-start.2
  136.8 0.8 copy-start.3
  169.8 0.8 copy-start
  206.1 1.0 copy-start.1

commit v3 on v2

v3 whole, which is shorter than its diff:
```python
import functools
import math

import jax
import jax.numpy as jnp
from jax import lax
from jax.experimental import pallas as pl
from jax.experimental.pallas import tpu as pltpu
from jax.sharding import PartitionSpec as P

TILE = 256
LANES = 128
CHUNK = 1024
GROUP = 16
BATCHES = 4
MESH = pl.DeviceIdType.MESH
NN = (((1,), (0,)), ((), ()))
NT = (((1,), (1,)), ((), ()))


def dot(a, b, dims):
    return lax.dot_general(a, b, dims, preferred_element_type=jnp.float32)


def spread_rows(dst, read, total):
    for k in range(total // LANES):
        row = read(k * LANES)
        dst[pl.ds(k * LANES, LANES), :] = jnp.broadcast_to(row, (LANES, LANES)).T


def gather_pieces(dst, src, pieces, width):
    for k in range(pieces):
        block, lane = (k * width) // TILE, (k * width) % TILE
        dst[block, :, lane : lane + width] = src(k)


def wide(column):
    return jnp.concatenate([column] * (TILE // LANES), axis=1)


def tile_pairs(blocks):
    return [(i, j) for i in range(blocks) for j in range(i, blocks)]


def add(held, term):
    return term if held is None else held + term


def multiply(sums, vec, tile, i, j):
    sums[j] = add(sums[j], dot(vec[i], tile, NN))
    if j > i:
        sums[i] = add(sums[i], dot(vec[j], tile, NT))


def keep_pieces(dst, slot, sums, pieces, width):
    for k in range(pieces):
        block, lane = (k * width) // TILE, (k * width) % TILE
        dst[slot, k] = sums[block][:, lane : lane + width].astype(dst.dtype)


def around(axis, count):
    me = lax.axis_index(axis)
    return me, [lax.rem(me + d, count) for d in range(1, count)]


def remote(axis, peer, src, dst, send, recv):
    return pltpu.make_async_remote_copy(
        src_ref=src,
        dst_ref=dst,
        send_sem=send,
        recv_sem=recv,
        device_id={axis: peer},
        device_id_type=MESH,
    )


def inward(axis, count, batch, sources, targets, send, recv):
    me, peers = around(axis, count)

    def copies(q):
        size = sources[0].shape[1] // batch
        at = pl.ds(q * size, size)
        return [
            remote(axis, peer, src.at[peer, at], dst.at[me, at], send.at[a, q, d], recv.at[a, q, d])
            for a, (src, dst) in enumerate(zip(sources, targets))
            for d, peer in enumerate(peers)
        ]

    return copies


def outward(axis, count, stage, landed, send, recv):
    me, peers = around(axis, count)

    def copies(w):
        return [
            remote(axis, peer, stage.at[w, peer], landed.at[me, w], send.at[w, d], recv.at[w, d])
            for d, peer in enumerate(peers)
        ]

    return copies


def open_batches(axis, count, batch, sources, targets, copies):
    me, _ = greet(axis, count)
    for q in range(batch):
        for copy in copies(q):
            copy.start()
    for src, dst in zip(sources, targets):
        dst[me] = src[me]


def close_all(own, batch, copies_in, copies_out):
    def sent(q, _):
        for copy in copies_in(q):
            copy.wait_send()
        return 0

    def done(w, _):
        for copy in copies_out(w):
            copy.wait()
        return 0

    lax.fori_loop(0, batch, sent, 0)
    lax.fori_loop(0, own, done, 0)


def forward_kernel(
    axis, pieces, width, own, batch,
    coords, profile, latent, kern, amp,
    dist, col_l, col_g, prof, vec, prof_all, draws_all, stage, landed,
    in_send, in_recv, out_send, out_recv,
):
    total = pieces * width
    pairs = tile_pairs(total // TILE)
    step = 64
    w = pl.program_id(0)
    sources, targets = (profile, latent), (prof_all, draws_all)
    copies_in = inward(axis, pieces, batch, sources, targets, in_send, in_recv)
    copies_out = outward(axis, pieces, stage, landed, out_send, out_recv)
    me = lax.axis_index(axis)

    @pl.when(w == 0)
    def _():
        open_batches(axis, pieces, batch, sources, targets, copies_in)
        spread_rows(col_l, lambda k: coords[0:1, k : k + LANES], total)
        spread_rows(col_g, lambda k: coords[1:2, k : k + LANES], total)

        def over_i(i, t0):
            def over_j(j, t):
                col = pl.ds(pl.multiple_of(j * TILE, TILE), TILE)
                x_c, y_c = coords[0:1, col], coords[1:2, col]
                for r in range(0, TILE, step):
                    row = pl.ds(pl.multiple_of(i * TILE + r, step), step)
                    dx = wide(col_l[row, :]) - x_c
                    dy = wide(col_g[row, :]) - y_c
                    dist[t, r : r + step, :] = (dx * dx + dy * dy) * (-math.log2(math.e))
                return t + 1

            return lax.fori_loop(i, total // TILE, over_j, t0)

        lax.fori_loop(0, total // TILE, over_i, 0)

    @pl.when(w > 0)
    def _():
        for copy in copies_out(w - 1):
            copy.start()
        landed[me, w - 1] = stage[w - 1, me]

    @pl.when(jnp.logical_and(w < own, lax.rem(w, own // batch) == 0))
    def _():
        for copy in copies_in(w // (own // batch)):
            copy.wait_recv()

    @pl.when(w < own)
    def _():
        gather_pieces(prof, lambda k: prof_all[k, w], pieces, width)
        gather_pieces(vec, lambda k: draws_all[k, w], pieces, width)
        spread_rows(col_l, lambda k: prof[k // TILE, 0:1, k % TILE : k % TILE + LANES], total)
        spread_rows(col_g, lambda k: prof[k // TILE, 1:2, k % TILE : k % TILE + LANES], total)
        sums = [None] * (total // TILE)
        for t, (i, j) in enumerate(pairs):
            l_c, g_c = prof[j, 0:1, :], prof[j, 1:2, :]
            strips = []
            for r in range(0, TILE, step):
                row = pl.ds(i * TILE + r, step)
                root = lax.rsqrt(wide(col_l[row, :]) + l_c)
                power = jnp.exp2(dist[t, r : r + step, :] * (root * root))
                scale = wide(col_g[row, :]) * g_c
                strip = (scale * root * power).astype(jnp.bfloat16)
                kern[0, t, r : r + step, :] = strip
                strips.append(strip)
            multiply(sums, vec, jnp.concatenate(strips, axis=0), i, j)
        keep_pieces(stage, w, sums, pieces, width)

    @pl.when(w == own)
    def _():
        close_all(own, batch, copies_in, copies_out)
        amp[...] = landed[...]


def backward_kernel(
    axis, pieces, width, own, batch,
    kern, grad, out,
    vec, grad_all, stage, landed, in_send, in_recv, out_send, out_recv,
):
    total = pieces * width
    w = pl.program_id(0)
    copies_in = inward(axis, pieces, batch, (grad,), (grad_all,), in_send, in_recv)
    copies_out = outward(axis, pieces, stage, landed, out_send, out_recv)
    me = lax.axis_index(axis)

    @pl.when(w == 0)
    def _():
        open_batches(axis, pieces, batch, (grad,), (grad_all,), copies_in)

    @pl.when(w > 0)
    def _():
        for copy in copies_out(w - 1):
            copy.start()
        landed[me, w - 1] = stage[w - 1, me]

    @pl.when(jnp.logical_and(w < own, lax.rem(w, own // batch) == 0))
    def _():
        for copy in copies_in(w // (own // batch)):
            copy.wait_recv()

    @pl.when(w < own)
    def _():
        gather_pieces(vec, lambda k: grad_all[k, w], pieces, width)
        sums = [None] * (total // TILE)
        for t, (i, j) in enumerate(tile_pairs(total // TILE)):
            multiply(sums, vec, kern[0, t], i, j)
        keep_pieces(stage, w, sums, pieces, width)

    @pl.when(w == own)
    def _():
        close_all(own, batch, copies_in, copies_out)
        out[...] = landed[...]


def field_kernel(samples, inner, first, last, rows, basis, label, field):
    base = pl.program_id(0) * inner

    def group(c, start):
        at = pl.ds(c * CHUNK, CHUNK)
        part = rows[pl.ds(pl.multiple_of(start * samples, 2 * samples), GROUP * samples), :]
        full = dot(part, basis[at, :], NT)
        own = jnp.broadcast_to(label[:, at], (samples, CHUNK)) - start
        total = jnp.zeros((samples, CHUNK), jnp.float32)
        for b in range(GROUP):
            total = total + jnp.where(own == b, full[b * samples : (b + 1) * samples, :], 0.0)
        return total

    starts = [first[base + c] // 2 * 2 for c in range(inner)]
    totals = [group(c, starts[c]) for c in range(inner)]
    for c in range(inner):
        trips = (last[base + c] - starts[c]) // GROUP + 1

        def over(k, total, c=c):
            return total + group(c, starts[c] + k * GROUP)

        total = lax.fori_loop(1, trips, over, totals[c])
        field[0, :, c * CHUNK : (c + 1) * CHUNK] = total.astype(field.dtype)


def sums_kernel(samples, inner, first, last, weight, basis, label, sums):
    base = pl.program_id(0) * inner

    @pl.when(pl.program_id(0) == 0)
    def _():
        sums[...] = jnp.zeros_like(sums)

    def group(c, start):
        at = pl.ds(c * CHUNK, CHUNK)
        own = jnp.broadcast_to(label[:, at], (samples, CHUNK)) - start
        value = weight[0, :, at].astype(jnp.float32)
        full = jnp.concatenate([jnp.where(own == b, value, 0.0) for b in range(GROUP)], axis=0)
        return dot(full.astype(jnp.bfloat16), basis[at, :], NN)

    def put(start, term):
        sums[pl.ds(pl.multiple_of(start * samples, 2 * samples), GROUP * samples), :] += term

    starts = [first[base + c] // 2 * 2 for c in range(inner)]
    terms = [group(c, starts[c]) for c in range(inner)]
    for c in range(inner):
        put(starts[c], terms[c])
    for c in range(inner):
        trips = (last[base + c] - starts[c]) // GROUP + 1

        def over(k, _, c=c):
            put(starts[c] + k * GROUP, group(c, starts[c] + k * GROUP))
            return 0

        lax.fori_loop(1, trips, over, 0)


def greet(axis, count):
    me = lax.axis_index(axis)
    peers = [lax.rem(me + d, count) for d in range(1, count)]
    barrier = pltpu.get_barrier_semaphore()
    for peer in peers:
        pl.semaphore_signal(barrier, inc=1, device_id={axis: peer}, device_id_type=MESH)
    pl.semaphore_wait(barrier, count - 1)
    return me, peers


def weight_kernel(axis, count, samples, partial, weight, landed, made, send, recv, local):
    me, peers = greet(axis, count)
    copies = []
    for d, peer in enumerate(peers):
        copy = pltpu.make_async_remote_copy(
            src_ref=partial.at[peer],
            dst_ref=landed.at[d],
            send_sem=send.at[0, d],
            recv_sem=recv.at[0, d],
            device_id={axis: peer},
            device_id_type=MESH,
        )
        copy.start()
        copies.append(copy)
    for copy in copies:
        copy.wait()
    total = partial[me].astype(jnp.float32)
    for d in range(count - 1):
        total = total + landed[d].astype(jnp.float32)
    made[...] = (-2.0 * total / (1.0 + total * total) / samples).astype(made.dtype)
    keep = pltpu.make_async_copy(made, weight.at[me], local)
    keep.start()
    keep.wait()
    copies = []
    for d, peer in enumerate(peers):
        copy = pltpu.make_async_remote_copy(
            src_ref=weight.at[me],
            dst_ref=weight.at[me],
            send_sem=send.at[1, d],
            recv_sem=recv.at[1, d],
            device_id={axis: peer},
            device_id_type=MESH,
        )
        copy.start()
        copies.append(copy)
    for copy in copies:
        copy.wait()


def share_weight(axis, count, ident, samples, partial):
    vmem = pl.BlockSpec(memory_space=pltpu.VMEM)
    shape, dtype = partial.shape, partial.dtype
    return pl.pallas_call(
        functools.partial(weight_kernel, axis, count, samples),
        out_shape=jax.ShapeDtypeStruct(shape, dtype),
        in_specs=[vmem],
        out_specs=vmem,
        scratch_shapes=[
            pltpu.VMEM((count - 1,) + shape[1:], dtype),
            pltpu.VMEM(shape[1:], dtype),
            pltpu.SemaphoreType.DMA((2, count - 1)),
            pltpu.SemaphoreType.DMA((2, count - 1)),
            pltpu.SemaphoreType.DMA,
        ],
        compiler_params=pltpu.CompilerParams(
            collective_id=ident, has_side_effects=True, vmem_limit_bytes=12 << 20
        ),
        name="share_weight",
    )(partial)


def params(**more):
    return pltpu.CompilerParams(
        dimension_semantics=("arbitrary",), vmem_limit_bytes=60 << 20, **more
    )


def shards(count, splits, latent, basis, event_bin, length, amplitude_scale, yield_norm, bin_coords):
    samples, waves, width = latent.shape
    total = bin_coords.shape[1]
    own = waves // count
    blocks = total // TILE
    tiles = blocks * (blocks + 1) // 2
    f32, bf16 = jnp.float32, jnp.bfloat16

    profile = jnp.stack(
        [length * length, amplitude_scale * jnp.sqrt(math.sqrt(2.0) * length)], axis=1
    ).reshape(count, own, 2, width)
    draws = jnp.transpose(latent, (1, 0, 2)).reshape(count, own, samples, width)

    batch = math.gcd(own, BATCHES)
    vmem = pl.BlockSpec(memory_space=pltpu.VMEM)
    piece = jax.ShapeDtypeStruct((count, own, samples, width), bf16)
    kern_spec = pl.BlockSpec((1, tiles, TILE, TILE), lambda w: (jnp.minimum(w, own - 1), 0, 0, 0))
    stages = [
        pltpu.VMEM((own, count, samples, width), bf16),
        pltpu.VMEM((count, own, samples, width), bf16),
    ]

    def semaphores(arrays):
        return [pltpu.SemaphoreType.DMA((arrays, batch, count - 1))] * 2 + [
            pltpu.SemaphoreType.DMA((own, count - 1))
        ] * 2

    kern, amp = pl.pallas_call(
        functools.partial(forward_kernel, "event", count, width, own, batch),
        out_shape=(jax.ShapeDtypeStruct((own, tiles, TILE, TILE), bf16), piece),
        grid=(own + 1,),
        in_specs=[vmem, vmem, vmem],
        out_specs=(kern_spec, vmem),
        scratch_shapes=[
            pltpu.VMEM((tiles, TILE, TILE), f32),
            pltpu.VMEM((total, LANES), f32),
            pltpu.VMEM((total, LANES), f32),
            pltpu.VMEM((blocks, 2, TILE), f32),
            pltpu.VMEM((blocks, samples, TILE), bf16),
            pltpu.VMEM((count, own, 2, width), f32),
            pltpu.VMEM((count, own, samples, width), bf16),
        ]
        + stages
        + semaphores(2),
        compiler_params=params(collective_id=0, has_side_effects=True),
        name="kern_forward",
    )(bin_coords, profile, draws)

    amp = amp.reshape(waves, samples, width)
    amp_rows = jnp.transpose(amp, (2, 1, 0)).reshape(width * samples, waves)
    amp_rows = jnp.pad(amp_rows, ((0, GROUP * samples), (0, 0)))

    events = basis.shape[0]
    block = min(events // splits, 4096)
    per = events // splits // block
    inner = block // CHUNK
    grouped = event_bin.reshape(events // CHUNK, CHUNK)
    first, last = grouped[:, 0], grouped[:, -1]
    basis_spec = pl.BlockSpec((block, waves), lambda e, *_: (e, 0))
    label_spec = pl.BlockSpec((1, block), lambda e, *_: (0, e))
    field_spec = pl.BlockSpec((1, samples, block), lambda e, *_: (e // per, 0, e % per))
    rows_spec = pl.BlockSpec(((width + GROUP) * samples, waves), lambda e, *_: (0, 0))
    field = pl.pallas_call(
        functools.partial(field_kernel, samples, inner),
        out_shape=jax.ShapeDtypeStruct((splits, samples, events // splits), bf16),
        grid_spec=pltpu.PrefetchScalarGridSpec(
            num_scalar_prefetch=2,
            grid=(events // block,),
            in_specs=[rows_spec, basis_spec, label_spec],
            out_specs=field_spec,
        ),
        compiler_params=params(),
        name="event_field",
    )(first, last, amp_rows, basis, event_bin)
    weight = share_weight("wave", splits, 2, samples, field)
    sums = pl.pallas_call(
        functools.partial(sums_kernel, samples, inner),
        out_shape=jax.ShapeDtypeStruct(((width + GROUP) * samples, waves), f32),
        grid_spec=pltpu.PrefetchScalarGridSpec(
            num_scalar_prefetch=2,
            grid=(events // block,),
            in_specs=[field_spec, basis_spec, label_spec],
            out_specs=rows_spec,
        ),
        compiler_params=params(),
        name="event_sums",
    )(first, last, weight, basis, event_bin)

    sums = jnp.transpose(sums[: width * samples].reshape(width, samples, waves), (2, 1, 0))
    grad = (sums + 2.0 / samples * amp.astype(f32) * yield_norm[:, None, :]).astype(bf16)
    pulled = pl.pallas_call(
        functools.partial(backward_kernel, "event", count, width, own, batch),
        out_shape=piece,
        grid=(own + 1,),
        in_specs=[kern_spec, vmem],
        out_specs=vmem,
        scratch_shapes=[
            pltpu.VMEM((blocks, samples, TILE), bf16),
            pltpu.VMEM((count, own, samples, width), bf16),
        ]
        + stages
        + semaphores(1),
        compiler_params=params(collective_id=1, has_side_effects=True),
        name="kern_backward",
    )(kern, grad.reshape(count, own, samples, width))
    pulled = pulled.reshape(waves, samples, width).astype(f32)
    return jnp.transpose(pulled, (1, 0, 2)) + latent.astype(f32)


def solution(mesh):
    placed = (
        P(None, "wave", "event"),
        P("event", "wave"),
        P("event", None),
        P("wave", "event"),
        P("wave", "event"),
        P("wave", "event"),
        P(),
    )
    return jax.shard_map(
        functools.partial(shards, mesh.shape["event"], mesh.shape["wave"]),
        mesh=mesh,
        in_specs=placed,
        out_specs=P(None, "wave", "event"),
        check_vma=False,
    )
```

time: 225 us -> 179 us (0.80)
  Pallas kernels: 205 us -> 161 us
    pallas_call x6 -> x2, Pallas kernels: 156 us -> 124 us  [the longest x1 75.1 us: shards(): pl.pallas_call(functools.partial(forward_kernel, 'event', count, width, o...]
    pallas_call x1, Pallas kernels: 15.3 us -> 9.28 us  [shards(): pl.pallas_call(functools.partial(field_kernel, samples, inner), out_shape...]
    pallas_call x1, Pallas kernels: 14.9 us -> 9.41 us  [shards(): pl.pallas_call(functools.partial(sums_kernel, samples, inner), out_shape=...]
    unnamed x17 -> x13, local copies, waits for them, and re-layouts: 6.75 us -> 3.53 us
where the time goes in v3:
time: 179 us; the launch traced here: 178 us
  Pallas kernels  161 us (90%)
  local copies, waits for them, and re-layouts  10.3 us (6%)
  other arithmetic  7.24 us (4%)
    pallas_call x1, Pallas kernels, shards(): pl.pallas_call(functools.partial(forward_kernel, 'event', count, width, o...  75.1 us
    pallas_call x1, Pallas kernels, shards(): pl.pallas_call(functools.partial(backward_kernel, 'event', count, width,...  48.9 us
    pallas_call x1, Pallas kernels, share_weight(): pl.pallas_call(functools.partial(weight_kernel, axis, count, samples), ou...  17.9 us
    pallas_call x1, Pallas kernels, shards(): pl.pallas_call(functools.partial(sums_kernel, samples, inner), out_shape=...  9.41 us
    pallas_call x1, Pallas kernels, shards(): pl.pallas_call(functools.partial(field_kernel, samples, inner), out_shape...  9.28 us

profile of v3, /device:TPU:0, one launch (start us, length us, event | category | flops | bytes accessed | tf_op | source)
XLA Modules:
  0.0 178.3 jit_solution(3710609123984904222)
XLA Ops:
  0.0 1.0 sqrt_multiply_fusion
  1.0 0.1 stack.10
  1.2 0.1 stack.9
  1.3 0.9 pad_maximum_fusion.profile
  2.2 2.1 %copy.8 = bf16[128,8,256]{2,1,0:T(8,128)(2,1)} copy(bf16[128,8,256]{2,0,1:T(8,128)(2,1)} %bitcast.22) | data formatting | bytes 1048576 | tf_op jit(solution)/shard_map/transpose | solution.py:386
  4.4 75.1 %kern_forward.1 = (bf16[16,36,256,256]{3,2,1,0:T(8,128)(2,1)}, bf16[8,16,8,256]{3,2,1,0:T(8,128)(2,1)}) custom-call(f32[2,2048]{1,0:T(2,128)} %coords.1, f32[8,16,2,256]{3,2,1,0:T(2,128)} %pad_maximum_fusion.profile, bf16[8,16,8,256]{3,2,1,0:T(8,128)(2,1)} %bitcast.24), custom_call_target="tpu_custom_call" | custom-call | tf_op jit(solution)/shard_map/kern_forward/pallas_call | solution.py:402
  79.5 0.5 broadcast.7
  80.0 1.9 %reduce.3 = s32[32768]{0:T(1024)S(1)} reduce(s32[1,32768]{1,0:T(1,128)} %label.3, s32[]{:T(128)} %broadcast.7), dimensions={0}, to_apply=%param.9.reduce_sub_computation.3 | reduce | bytes 262148 | tf_op args[2]
  81.9 0.1 fusion.1
  82.0 0.6 copy.14
  82.6 0.6 copy.15
  83.2 1.6 copy.11
  84.8 0.8 pad.4.rows
  85.6 9.3 %event_field.1.partial = bf16[4,8,8192]{2,1,0:T(8,128)(2,1)} custom-call(s32[32]{0:T(128)} %bitcast.26, s32[32]{0:T(128)} %bitcast.28, bf16[2176,128]{1,0:T(8,128)(2,1)} %pad.4.rows, bf16[32768,128]{1,0:T(8,128)(2,1)} %basis.3, s32[1,32768]{1,0:T(1,128)} %label.3), custom_call_target="tpu_custom_call" | custom-call | tf_op jit(solution)/shard_map/event_field/pallas_call | solution.py:437
  94.9 0.0 copy-start
  94.9 1.0 copy-done
  96.0 0.0 copy-start.4
  96.0 0.0 copy-start.3
  96.0 17.9 %share_weight.1.weight = bf16[4,8,8192]{2,1,0:T(8,128)(2,1)S(1)} custom-call(bf16[4,8,8192]{2,1,0:T(8,128)(2,1)S(1)} %copy-done), custom_call_target="tpu_custom_call" | custom-call | tf_op jit(solution)/shard_map/share_weight/pallas_call | solution.py:350
  113.9 0.0 copy-start.1
  113.9 0.8 copy-done.1
  114.6 9.4 %event_sums.1 = f32[2176,128]{1,0:T(8,128)} custom-call(s32[32]{0:T(128)} %bitcast.27, s32[32]{0:T(128)} %bitcast.29, bf16[4,8,8192]{2,1,0:T(8,128)(2,1)} %copy-done.1, bf16[32768,128]{1,0:T(8,128)(2,1)} %basis.3, s32[1,32768]{1,0:T(1,128)} %label.3), custom_call_target="tpu_custom_call" | custom-call | tf_op jit(solution)/shard_map/event_sums/pallas_call | solution.py:450
  124.1 1.3 slice_bitcast_fusion
  125.4 0.6 copy.12
  125.9 0.0 copy-done.4
  126.0 0.0 copy-done.3
  126.0 1.0 fusion
  126.9 0.0 copy-start.2
  126.9 48.9 %kern_backward.1 = bf16[8,16,8,256]{3,2,1,0:T(8,128)(2,1)} custom-call(bf16[16,36,256,256]{3,2,1,0:T(8,128)(2,1)} %get-tuple-element.7.kern, bf16[8,16,8,256]{3,2,1,0:T(8,128)(2,1)} %bitcast.21), custom_call_target="tpu_custom_call" | custom-call | tf_op jit(solution)/shard_map/kern_backward/pallas_call | solution.py:465
  175.9 1.1 bitcast_convert_fusion
  177.0 0.0 copy-done.2
  177.0 1.3 bitcast_add_fusion
  (2 shorter events, 0.0 us)
Async XLA Ops:
  94.9 1.0 copy-start
  96.0 30.0 %copy-start.4 = (f32[128,256]{1,0:T(8,128)S(1)}, f32[128,256]{1,0:T(8,128)}, u32[]{:S(2)}) copy-start(f32[128,256]{1,0:T(8,128)} %param.12) | copy-start | bytes 393220
  96.0 30.0 %copy-start.3 = (bf16[8,16,8,256]{3,2,1,0:T(8,128)(2,1)S(1)}, bf16[8,16,8,256]{3,2,1,0:T(8,128)(2,1)}, u32[]{:S(2)}) copy-start(bf16[8,16,8,256]{3,2,1,0:T(8,128)(2,1)} %get-tuple-element.8) | copy-start | bytes 1572868
  113.9 0.8 copy-start.1
  126.9 50.1 %copy-start.2 = (bf16[8,128,256]{2,1,0:T(8,128)(2,1)S(1)}, bf16[8,128,256]{2,1,0:T(8,128)(2,1)}, u32[]{:S(2)}) copy-start(bf16[8,128,256]{2,1,0:T(8,128)(2,1)} %param.7) | copy-start | bytes 1572868

commit v4 on v3

--- a/solution.py
+++ b/solution.py
@@ -12,7 +12,7 @@
 LANES = 128
 CHUNK = 1024
 GROUP = 16
-BATCHES = 4
+BATCHES = 8
 MESH = pl.DeviceIdType.MESH
 NN = (((1,), (0,)), ((), ()))
 NT = (((1,), (1,)), ((), ()))

time: 179 us -> 177 us (0.989)
  Pallas kernels: 161 us -> 158 us
where the time goes in v4:
time: 177 us; the launch traced here: 176 us
  Pallas kernels  158 us (89%)
  local copies, waits for them, and re-layouts  10.3 us (6%)
  other arithmetic  7.24 us (4%)
    pallas_call x1, Pallas kernels, shards(): pl.pallas_call(functools.partial(forward_kernel, 'event', count, width, o...  74 us
    pallas_call x1, Pallas kernels, shards(): pl.pallas_call(functools.partial(backward_kernel, 'event', count, width,...  48.1 us
    pallas_call x1, Pallas kernels, share_weight(): pl.pallas_call(functools.partial(weight_kernel, axis, count, samples), ou...  17.7 us
    pallas_call x1, Pallas kernels, shards(): pl.pallas_call(functools.partial(sums_kernel, samples, inner), out_shape=...  9.41 us
    pallas_call x1, Pallas kernels, shards(): pl.pallas_call(functools.partial(field_kernel, samples, inner), out_shape...  9.28 us

profile of v4, /device:TPU:0, one launch (start us, length us, event | category | flops | bytes accessed | tf_op | source)
XLA Modules:
  0.0 176.2 jit_solution(14584963947607118460)
XLA Ops:
  0.0 1.0 sqrt_multiply_fusion
  1.0 0.1 stack.10
  1.2 0.1 stack.9
  1.3 0.9 pad_maximum_fusion.profile
  2.2 2.1 %copy.8 = bf16[128,8,256]{2,1,0:T(8,128)(2,1)} copy(bf16[128,8,256]{2,0,1:T(8,128)(2,1)} %bitcast.22) | data formatting | bytes 1048576 | tf_op jit(solution)/shard_map/transpose | solution.py:386
  4.4 74.0 %kern_forward.1 = (bf16[16,36,256,256]{3,2,1,0:T(8,128)(2,1)}, bf16[8,16,8,256]{3,2,1,0:T(8,128)(2,1)}) custom-call(f32[2,2048]{1,0:T(2,128)} %coords.1, f32[8,16,2,256]{3,2,1,0:T(2,128)} %pad_maximum_fusion.profile, bf16[8,16,8,256]{3,2,1,0:T(8,128)(2,1)} %bitcast.24), custom_call_target="tpu_custom_call" | custom-call | tf_op jit(solution)/shard_map/kern_forward/pallas_call | solution.py:402
  78.4 0.5 broadcast.7
  78.9 1.9 %reduce.3 = s32[32768]{0:T(1024)S(1)} reduce(s32[1,32768]{1,0:T(1,128)} %label.3, s32[]{:T(128)} %broadcast.7), dimensions={0}, to_apply=%param.9.reduce_sub_computation.3 | reduce | bytes 262148 | tf_op args[2]
  80.8 0.1 fusion.1
  80.9 0.6 copy.14
  81.5 0.6 copy.15
  82.1 1.6 copy.11
  83.7 0.8 pad.4.rows
  84.5 9.3 %event_field.1.partial = bf16[4,8,8192]{2,1,0:T(8,128)(2,1)} custom-call(s32[32]{0:T(128)} %bitcast.26, s32[32]{0:T(128)} %bitcast.28, bf16[2176,128]{1,0:T(8,128)(2,1)} %pad.4.rows, bf16[32768,128]{1,0:T(8,128)(2,1)} %basis.3, s32[1,32768]{1,0:T(1,128)} %label.3), custom_call_target="tpu_custom_call" | custom-call | tf_op jit(solution)/shard_map/event_field/pallas_call | solution.py:437
  93.8 0.0 copy-start
  93.8 1.0 copy-done
  94.9 0.0 copy-start.4
  94.9 0.0 copy-start.3
  94.9 17.7 %share_weight.1.weight = bf16[4,8,8192]{2,1,0:T(8,128)(2,1)S(1)} custom-call(bf16[4,8,8192]{2,1,0:T(8,128)(2,1)S(1)} %copy-done), custom_call_target="tpu_custom_call" | custom-call | tf_op jit(solution)/shard_map/share_weight/pallas_call | solution.py:350
  112.6 0.0 copy-start.1
  112.6 0.8 copy-done.1
  113.4 9.4 %event_sums.1 = f32[2176,128]{1,0:T(8,128)} custom-call(s32[32]{0:T(128)} %bitcast.27, s32[32]{0:T(128)} %bitcast.29, bf16[4,8,8192]{2,1,0:T(8,128)(2,1)} %copy-done.1, bf16[32768,128]{1,0:T(8,128)(2,1)} %basis.3, s32[1,32768]{1,0:T(1,128)} %label.3), custom_call_target="tpu_custom_call" | custom-call | tf_op jit(solution)/shard_map/event_sums/pallas_call | solution.py:450
  122.8 1.3 slice_bitcast_fusion
  124.1 0.6 copy.12
  124.6 0.0 copy-done.4
  124.7 0.0 copy-done.3
  124.7 1.0 fusion
  125.7 0.0 copy-start.2
  125.7 48.1 %kern_backward.1 = bf16[8,16,8,256]{3,2,1,0:T(8,128)(2,1)} custom-call(bf16[16,36,256,256]{3,2,1,0:T(8,128)(2,1)} %get-tuple-element.7.kern, bf16[8,16,8,256]{3,2,1,0:T(8,128)(2,1)} %bitcast.21), custom_call_target="tpu_custom_call" | custom-call | tf_op jit(solution)/shard_map/kern_backward/pallas_call | solution.py:465
  173.8 1.1 bitcast_convert_fusion
  174.9 0.0 copy-done.2
  174.9 1.3 bitcast_add_fusion
  (2 shorter events, 0.0 us)
Async XLA Ops:
  93.8 1.0 copy-start
  94.9 29.8 %copy-start.4 = (f32[128,256]{1,0:T(8,128)S(1)}, f32[128,256]{1,0:T(8,128)}, u32[]{:S(2)}) copy-start(f32[128,256]{1,0:T(8,128)} %param.12) | copy-start | bytes 393220
  94.9 29.8 %copy-start.3 = (bf16[8,16,8,256]{3,2,1,0:T(8,128)(2,1)S(1)}, bf16[8,16,8,256]{3,2,1,0:T(8,128)(2,1)}, u32[]{:S(2)}) copy-start(bf16[8,16,8,256]{3,2,1,0:T(8,128)(2,1)} %get-tuple-element.8) | copy-start | bytes 1572868
  112.6 0.8 copy-start.1
  125.7 49.2 %copy-start.2 = (bf16[8,128,256]{2,1,0:T(8,128)(2,1)S(1)}, bf16[8,128,256]{2,1,0:T(8,128)(2,1)}, u32[]{:S(2)}) copy-start(bf16[8,128,256]{2,1,0:T(8,128)(2,1)} %param.7) | copy-start | bytes 1572868
